TPU v7x, 128 devices: a whole 4x4x4 slice. The times are simulated.
128 devices in a mesh: row: 32 (over x, y, core), col: 4 (over z).
Axes of the slice: x: 4, y: 4, z: 4, core: 2. Of those that a mesh axis runs over, the one named last changes fastest.
Arguments:
- front_matrix: float32 [12288, 16384], P('row', 'col'), may hold values from -6 to 6
- child_rows: float32 [2048, 16384], P('row', 'col'), may hold values from -6 to 6
- child_owner: int32 [2048, 1], P('row'), may hold values from 0 to 31; in each aligned block of 64 rows (0 to 63, 64 to 127, ...) at most 4 rows name the same one
- child_offset: int32 [2048, 1], P('row'), may hold values from 0 to 383
Outputs:
- upper_rows: float32 [512, 16384], P(None, 'col')
- reduced_front: float32 [12288, 16384], P('row', 'col')
- basis_scaled: float32 [12288, 512], P('row')
Inputs may be any that keep to these rules, and one draw needn't show every extreme that they name: `child_owner`: within the rows of one device (aligned blocks of 64 rows) no value occurs more than 4 times, and some value occurs exactly 4 times.
All inputs are finite; a program needn't handle non-finite values.
Results may differ from a plain program's by a relative error of at most 0.0001.
Values sent between devices are 32-bit elements; how exact they have to be, the bound alone decides.
A program may use at most 128 MiB of HBM per device.

v0:
```python
import math

import jax
import jax.numpy as jnp
from jax import lax
from jax.sharding import PartitionSpec as P

PB = 128
PANELS = 4


def spread(block, axis, owner):
    block = jnp.where(lax.axis_index(axis) == owner, block, jnp.zeros_like(block))
    return lax.psum(block, axis)


def product(left_op, right_op):
    return jnp.dot(
        left_op, right_op, precision=lax.Precision.HIGHEST, preferred_element_type=jnp.float32
    )


def factor_panel(panel_cols):
    gram_part = product(panel_cols.T, panel_cols)
    gram_total = lax.psum(gram_part, "row")
    lower_factor = jnp.linalg.cholesky(gram_total)
    basis = lax.linalg.triangular_solve(
        lower_factor, panel_cols, left_side=False, lower=True, transpose_a=True
    )
    return spread(basis, "col", 0)


def on_device(front_matrix, child_rows, child_owner, child_offset):
    row_count = lax.axis_size("row")
    local_rows = front_matrix.shape[0]
    local_cols = front_matrix.shape[1]
    child_count = child_rows.shape[0]
    capacity = 2 * child_count // row_count
    slot_total = row_count * capacity
    owner_rows = child_owner[:, 0]
    onehot = (owner_rows[:, None] == jnp.arange(row_count, dtype=jnp.int32)[None, :]).astype(
        jnp.int32
    )
    rank_in = jnp.sum(onehot * (jnp.cumsum(onehot, axis=0) - 1), axis=1)
    position = owner_rows * capacity + rank_in
    sender = jnp.zeros((slot_total, local_cols), jnp.float32).at[position].set(child_rows)
    offsets = jnp.full((slot_total,), local_rows, jnp.int32).at[position].set(child_offset[:, 0])
    received, placed = (
        lax.all_to_all(
            sender.reshape(row_count, capacity, local_cols),
            "row",
            split_axis=0,
            concat_axis=0,
            tiled=True,
        ),
        lax.all_to_all(
            offsets.reshape(row_count, capacity), "row", split_axis=0, concat_axis=0, tiled=True
        ),
    )
    current = front_matrix.at[placed.reshape(slot_total)].add(
        received.reshape(slot_total, local_cols), mode="drop"
    )
    top_list = []
    basis_list = []
    for panel_index in range(PANELS):
        basis = factor_panel(current[:, panel_index * PB : (panel_index + 1) * PB])
        top_rows = lax.psum(product(basis.T, current), "row")
        current = current - product(basis, top_rows)
        top_list.append(top_rows)
        basis_list.append(basis)
    total_rows = local_rows * row_count
    scaled = jnp.concatenate(basis_list, axis=1) * math.sqrt(total_rows)
    return (jnp.concatenate(top_list, axis=0), current, scaled)


def solution(mesh):
    placed = (P("row", "col"), P("row", "col"), P("row", None), P("row", None))
    return jax.shard_map(
        on_device,
        mesh=mesh,
        in_specs=placed,
        out_specs=(P(None, "col"), P("row", "col"), P("row", None)),
        check_vma=False,
    )
```

profile of v0, /device:TPU:1, one launch (start us, length us, event | category | flops | bytes accessed | tf_op | source)
XLA Modules:
  0.0 1253.9 jit_solution(3829371774254167464)
XLA Ops:
  15.4 8.6 all-to-all-start
  37.2 27.1 %all-to-all-done.1 = f32[32,4,4096]{2,1,0:T(4,128)} async-done(((f32[32,4,4096]{2,1,0:T(4,128)}), f32[32,4,4096]{2,1,0:T(4,128)}, u32[]{:S(2)}, u32[]{:S(2)}) %all-to-all-start.1) | async-done | bytes 2097184 | tf_op jit(solution)/shard_map/all_to_all | solution.py:49
  66.3 8.7 scatter_fusion
  77.4 95.6 %all-reduce.13.cloned.1.call-done = f32[128,128]{0,1:T(8,128)} async-done(((f32[128,128]{0,1:T(8,128)}), f32[128,128]{0,1:T(8,128)}) %all-reduce.13.cloned.1.call-update) | async-done | bytes 65552 | tf_op jit(solution)/shard_map/psum | solution.py:25
  174.7 11.7 cholesky.74
  187.8 9.8 custom-call.8
  199.7 38.5 %all-reduce.15.cloned.1.call-done = f32[384,128]{0,1:T(8,128)} async-done(((f32[384,128]{0,1:T(8,128)}), f32[384,128]{0,1:T(8,128)}) %all-reduce.15.cloned.1.call-update) | async-done | bytes 196624 | tf_op jit(solution)/shard_map/psum | solution.py:14
  246.6 109.6 %all-reduce.17.cloned.1.call-done = f32[128,4096]{1,0:T(8,128)} async-done(((f32[128,4096]{1,0:T(8,128)}), f32[128,4096]{1,0:T(8,128)}) %all-reduce.17.cloned.1.call-update) | async-done | bytes 2097168 | tf_op jit(solution)/shard_map/psum | solution.py:67
  368.0 97.3 %all-reduce.19.cloned.1.call-done = f32[128,128]{0,1:T(8,128)} async-done(((f32[128,128]{0,1:T(8,128)}), f32[128,128]{0,1:T(8,128)}) %all-reduce.19.cloned.1.call-update) | async-done | bytes 65552 | tf_op jit(solution)/shard_map/psum | solution.py:25
  467.1 11.7 cholesky.85
  480.2 9.8 custom-call.9
  492.1 38.5 %all-reduce.21.cloned.1.call-done = f32[384,128]{0,1:T(8,128)} async-done(((f32[384,128]{0,1:T(8,128)}), f32[384,128]{0,1:T(8,128)}) %all-reduce.21.cloned.1.call-update) | async-done | bytes 196624 | tf_op jit(solution)/shard_map/psum | solution.py:14
  538.8 109.8 %all-reduce.23.cloned.1.call-done = f32[128,4096]{1,0:T(8,128)} async-done(((f32[128,4096]{1,0:T(8,128)}), f32[128,4096]{1,0:T(8,128)}) %all-reduce.23.cloned.1.call-update) | async-done | bytes 2097168 | tf_op jit(solution)/shard_map/psum | solution.py:67
  660.8 96.8 %all-reduce.25.cloned.1.call-done = f32[128,128]{0,1:T(8,128)} async-done(((f32[128,128]{0,1:T(8,128)}), f32[128,128]{0,1:T(8,128)}) %all-reduce.25.cloned.1.call-update) | async-done | bytes 65552 | tf_op jit(solution)/shard_map/psum | solution.py:25
  759.4 11.7 cholesky.96
  772.5 9.8 custom-call.10
  784.4 38.5 %all-reduce.27.cloned.1.call-done = f32[384,128]{0,1:T(8,128)} async-done(((f32[384,128]{0,1:T(8,128)}), f32[384,128]{0,1:T(8,128)}) %all-reduce.27.cloned.1.call-update) | async-done | bytes 196624 | tf_op jit(solution)/shard_map/psum | solution.py:14
  831.2 109.6 %all-reduce.29.cloned.1.call-done = f32[128,4096]{1,0:T(8,128)} async-done(((f32[128,4096]{1,0:T(8,128)}), f32[128,4096]{1,0:T(8,128)}) %all-reduce.29.cloned.1.call-update) | async-done | bytes 2097168 | tf_op jit(solution)/shard_map/psum | solution.py:67
  952.7 97.2 %all-reduce.31.cloned.1.call-done = f32[128,128]{0,1:T(8,128)} async-done(((f32[128,128]{0,1:T(8,128)}), f32[128,128]{0,1:T(8,128)}) %all-reduce.31.cloned.1.call-update) | async-done | bytes 65552 | tf_op jit(solution)/shard_map/psum | solution.py:25
  1051.7 11.7 cholesky.107
  1064.7 9.8 custom-call.11
  1076.8 38.3 %all-reduce.33.cloned.1.call-done = f32[384,128]{0,1:T(8,128)} async-done(((f32[384,128]{0,1:T(8,128)}), f32[384,128]{0,1:T(8,128)}) %all-reduce.33.cloned.1.call-update) | async-done | bytes 196624 | tf_op jit(solution)/shard_map/psum | solution.py:14
  1124.5 108.6 %all-reduce.35.cloned.1.call-done = f32[128,4096]{1,0:T(8,128)} async-done(((f32[128,4096]{1,0:T(8,128)}), f32[128,4096]{1,0:T(8,128)}) %all-reduce.35.cloned.1.call-update) | async-done | bytes 2097168 | tf_op jit(solution)/shard_map/psum | solution.py:67
  1233.1 9.9 convolution_subtract_fusion
  (102 shorter events, 120.7 us)
Async XLA Ops:
  7.2 6.2 copy-start.11
  15.4 15.5 %all-to-all-start = ((s32[32,1,4]{2,1,0:T(1,128)}), s32[32,1,4]{2,1,0:T(1,128)S(1)}, u32[]{:S(2)}, u32[]{:S(2)}) async-start(s32[32,1,4]{2,1,0:T(1,128)} %bitcast.4), calls=%async_computation | async-start | bytes 32768 | tf_op jit(solution)/shard_map/all_to_all | solution.py:56
  30.8 33.5 %all-to-all-start.1 = ((f32[32,4,4096]{2,1,0:T(4,128)}), f32[32,4,4096]{2,1,0:T(4,128)}, u32[]{:S(2)}, u32[]{:S(2)}) async-start(f32[32,4,4096]{2,1,0:T(4,128)} %reshape.61), calls=%async_computation.1 | async-start | bytes 4194304 | tf_op jit(solution)/shard_map/all_to_all | solution.py:49
  35.9 137.1 %all-reduce.13.cloned.1.call-start = ((), (), s32[]{:S(2)}) async-start(), calls=%async_computation.2 | async-start | bytes 131072 | tf_op jit(solution)/shard_map/psum | solution.py:25
  77.1 161.1 %all-reduce.15.cloned.1.call-start = ((), (), s32[]{:S(2)}) async-start(), calls=%async_computation.3 | async-start | bytes 393216 | tf_op jit(solution)/shard_map/psum | solution.py:14
  199.6 156.5 %all-reduce.17.cloned.1.call-start = ((), (), s32[]{:S(2)}) async-start(), calls=%async_computation.4 | async-start | bytes 4194304 | tf_op jit(solution)/shard_map/psum | solution.py:67
  238.2 117.9 %copy-start.7 = (f32[384,128]{0,1:T(8,128)S(1)}, f32[384,128]{0,1:T(8,128)}, u32[]{:S(2)}) copy-start(f32[384,128]{0,1:T(8,128)} %all-reduce.15.cloned.1.call-done) | copy-start | bytes 589828
  246.3 219.0 %all-reduce.19.cloned.1.call-start = ((), (), s32[]{:S(2)}) async-start(), calls=%async_computation.5 | async-start | bytes 131072 | tf_op jit(solution)/shard_map/psum | solution.py:25
  364.1 2.7 copy-start.1
  368.0 162.6 %all-reduce.21.cloned.1.call-start = ((), (), s32[]{:S(2)}) async-start(), calls=%async_computation.6 | async-start | bytes 393216 | tf_op jit(solution)/shard_map/psum | solution.py:14
  492.0 156.5 %all-reduce.23.cloned.1.call-start = ((), (), s32[]{:S(2)}) async-start(), calls=%async_computation.7 | async-start | bytes 4194304 | tf_op jit(solution)/shard_map/psum | solution.py:67
  530.6 117.9 %copy-start.8 = (f32[384,128]{0,1:T(8,128)S(1)}, f32[384,128]{0,1:T(8,128)}, u32[]{:S(2)}) copy-start(f32[384,128]{0,1:T(8,128)} %all-reduce.21.cloned.1.call-done) | copy-start | bytes 589828
  538.7 218.9 %all-reduce.25.cloned.1.call-start = ((), (), s32[]{:S(2)}) async-start(), calls=%async_computation.8 | async-start | bytes 131072 | tf_op jit(solution)/shard_map/psum | solution.py:25
  660.4 162.5 %all-reduce.27.cloned.1.call-start = ((), (), s32[]{:S(2)}) async-start(), calls=%async_computation.9 | async-start | bytes 393216 | tf_op jit(solution)/shard_map/psum | solution.py:14
  784.3 156.5 %all-reduce.29.cloned.1.call-start = ((), (), s32[]{:S(2)}) async-start(), calls=%async_computation.10 | async-start | bytes 4194304 | tf_op jit(solution)/shard_map/psum | solution.py:67
  822.9 117.9 %copy-start.9 = (f32[384,128]{0,1:T(8,128)S(1)}, f32[384,128]{0,1:T(8,128)}, u32[]{:S(2)}) copy-start(f32[384,128]{0,1:T(8,128)} %all-reduce.27.cloned.1.call-done) | copy-start | bytes 589828
  831.0 218.9 %all-reduce.31.cloned.1.call-start = ((), (), s32[]{:S(2)}) async-start(), calls=%async_computation.11 | async-start | bytes 131072 | tf_op jit(solution)/shard_map/psum | solution.py:25
  952.6 162.5 %all-reduce.33.cloned.1.call-start = ((), (), s32[]{:S(2)}) async-start(), calls=%async_computation.12 | async-start | bytes 393216 | tf_op jit(solution)/shard_map/psum | solution.py:14
  1076.6 156.5 %all-reduce.35.cloned.1.call-start = ((), (), s32[]{:S(2)}) async-start(), calls=%async_computation.13 | async-start | bytes 4194304 | tf_op jit(solution)/shard_map/psum | solution.py:67
  1115.1 8.1 copy-start.10
  1124.5 118.5 %copy-start.3 = (f32[128,4096]{1,0:T(8,128)S(1)}, f32[128,4096]{1,0:T(8,128)}, u32[]{:S(2)}) copy-start(f32[128,4096]{1,0:T(8,128)} %all-reduce.17.cloned.1.call-done) | copy-start | bytes 6291460
  1233.1 9.9 copy-start.4
  1233.1 9.9 copy-start.5
  1233.1 9.9 copy-start.6
  (2 other events, 5.4 us)
Sparse Core Ops, SparseCore 0:
  77.3 95.6 all-reduce.12
  199.8 38.4 all-reduce.14
  246.4 109.6 all-reduce.16
  368.1 97.1 all-reduce.18
  492.1 38.4 all-reduce.20
  538.8 109.6 all-reduce.22
  660.5 97.0 all-reduce.24
  784.4 38.4 all-reduce.26
  831.1 109.6 all-reduce.28
  952.7 97.1 all-reduce.30
  1076.7 38.4 all-reduce.32
  1123.4 109.6 all-reduce.34
where the time goes:
time: 1260 us; the launch traced here: 1250 us
  waiting for transfers between devices  1010 us (80%)
  other arithmetic  108 us (9%)
  matrix products  79.6 us (6%)
  local copies, waits for them, and re-layouts  27.4 us (2%)
  starting transfers between devices  15.3 us (1%)
  between operations  14.7 us (1%)
    psum x4, waiting for transfers between devices, on_device(): top_rows = lax.psum(product(basis.T, current), 'row')  437 us
    psum x4, waiting for transfers between devices, factor_panel(): gram_total = lax.psum(gram_part, 'row')  387 us
    psum x4, waiting for transfers between devices, spread(): return lax.psum(block, axis)  154 us
    dot_general x12, matrix products, product(): jnp.dot(left_op, right_op, precision=lax.Precision.HIGHEST, preferred_ele...  71.6 us
    another operation x12, other arithmetic, factor_panel(): lower_factor = jnp.linalg.cholesky(gram_total)  49.6 us
    another operation x8, other arithmetic, factor_panel(): lax.linalg.triangular_solve(lower_factor, panel_cols, left_side=False, lo...  41.9 us
    all_to_all x1, waiting for transfers between devices, on_device(): lax.all_to_all(sender.reshape(row_count, capacity, local_cols), 'row', sp...  27.1 us
  transfers between devices with their start and end apart: 14, of which 14 were waited for; matrix products, arithmetic and copies ran while one was open for 1% of the time, Pallas kernels for 0%

commit v1 on v0

--- a/solution.py
+++ b/solution.py
@@ -7,11 +7,7 @@
 
 PB = 128
 PANELS = 4
-
-
-def spread(block, axis, owner):
-    block = jnp.where(lax.axis_index(axis) == owner, block, jnp.zeros_like(block))
-    return lax.psum(block, axis)
+WIDE = PB * PANELS
 
 
 def product(left_op, right_op):
@@ -20,14 +16,14 @@
     )
 
 
-def factor_panel(panel_cols):
-    gram_part = product(panel_cols.T, panel_cols)
-    gram_total = lax.psum(gram_part, "row")
-    lower_factor = jnp.linalg.cholesky(gram_total)
-    basis = lax.linalg.triangular_solve(
-        lower_factor, panel_cols, left_side=False, lower=True, transpose_a=True
-    )
-    return spread(basis, "col", 0)
+def from_first(block, axis):
+    count = lax.axis_size(axis)
+    me = lax.axis_index(axis)
+    out = block
+    for peer in range(1, count):
+        got = lax.ppermute(block, axis, [(0, peer)])
+        out = jnp.where(me == peer, got, out)
+    return out
 
 
 def on_device(front_matrix, child_rows, child_owner, child_offset):
@@ -60,17 +56,18 @@
     current = front_matrix.at[placed.reshape(slot_total)].add(
         received.reshape(slot_total, local_cols), mode="drop"
     )
-    top_list = []
-    basis_list = []
-    for panel_index in range(PANELS):
-        basis = factor_panel(current[:, panel_index * PB : (panel_index + 1) * PB])
-        top_rows = lax.psum(product(basis.T, current), "row")
-        current = current - product(basis, top_rows)
-        top_list.append(top_rows)
-        basis_list.append(basis)
+    panel = from_first(current[:, :WIDE], "col")
+    inner = lax.psum(product(panel.T, current), "row")
+    gram = from_first(inner[:, :WIDE], "col")
+    lower_factor = jnp.linalg.cholesky(gram)
+    inverse = lax.linalg.triangular_solve(
+        lower_factor, jnp.eye(WIDE, dtype=jnp.float32), left_side=True, lower=True
+    )
+    upper = product(inverse, inner)
+    basis = product(panel, inverse.T)
+    reduced = current - product(basis, upper)
     total_rows = local_rows * row_count
-    scaled = jnp.concatenate(basis_list, axis=1) * math.sqrt(total_rows)
-    return (jnp.concatenate(top_list, axis=0), current, scaled)
+    return (upper, reduced, basis * math.sqrt(total_rows))
 
 
 def solution(mesh):

time: 1260 us -> 502 us (0.40)
  waiting for transfers between devices: 1010 us -> 218 us
  other arithmetic: 108 us -> 134 us
  matrix products: 79.6 us -> 60 us
  starting transfers between devices: 15.3 us -> 31.8 us
    psum x12 -> x1, waiting for transfers between devices: 978 us -> 118 us  [on_device(): inner = lax.psum(product(panel.T, current), 'row')]
    ppermute x0 -> x6, waiting for transfers between devices: none -> 70.5 us  [from_first(): got = lax.ppermute(block, axis, [(0, peer)])]
    another operation x20 -> x17, other arithmetic: 91.4 us -> 120 us  [the longest x14 78.8 us: on_device(): lower_factor = jnp.linalg.cholesky(gram)]
    dot_general x12 -> x4, matrix products: 71.6 us -> 48.9 us  [product(): jnp.dot(left_op, right_op, precision=lax.Precision.HIGHEST, preferred_ele...]
    ppermute x0 -> x6, starting transfers between devices: none -> 18.2 us  [from_first(): got = lax.ppermute(block, axis, [(0, peer)])]
    another operation x0 -> x17, local copies, waits for them, and re-layouts: none -> 14.5 us
  transfers between devices with their start and end apart: 14 -> 9, of which waited for: 14 -> 9; matrix products, arithmetic and copies ran while one was open for 1% -> 1% of each run, Pallas kernels for 0% -> 0%
where the time goes in v1:
time: 502 us; the launch traced here: 495 us
  waiting for transfers between devices  218 us (43%)
  other arithmetic  134 us (27%)
  matrix products  60 us (12%)
  local copies, waits for them, and re-layouts  32.7 us (7%)
  starting transfers between devices  31.8 us (6%)
  between operations  17.4 us (3%)
    psum x1, waiting for transfers between devices, on_device(): inner = lax.psum(product(panel.T, current), 'row')  118 us
    another operation x14, other arithmetic, on_device(): lower_factor = jnp.linalg.cholesky(gram)  78.8 us
    ppermute x6, waiting for transfers between devices, from_first(): got = lax.ppermute(block, axis, [(0, peer)])  70.5 us
    dot_general x4, matrix products, product(): jnp.dot(left_op, right_op, precision=lax.Precision.HIGHEST, preferred_ele...  48.9 us
    another operation x3, other arithmetic, on_device(): lax.linalg.triangular_solve(lower_factor, jnp.eye(WIDE, dtype=jnp.float32...  41.2 us
    all_to_all x1, waiting for transfers between devices, on_device(): lax.all_to_all(sender.reshape(row_count, capacity, local_cols), 'row', sp...  27.1 us
    ppermute x6, starting transfers between devices, from_first(): got = lax.ppermute(block, axis, [(0, peer)])  18.2 us
    another operation x12, local copies, waits for them, and re-layouts  14.3 us
  transfers between devices with their start and end apart: 9, of which 9 were waited for; matrix products, arithmetic and copies ran while one was open for 1% of the time, Pallas kernels for 0%

profile of v1, /device:TPU:1, one launch (start us, length us, event | category | flops | bytes accessed | tf_op | source)
XLA Modules:
  0.0 494.7 jit_solution(10586973095307665705)
XLA Ops:
  7.2 6.2 %copy.33 = f32[384,4096]{1,0:T(8,128)} copy(f32[384,4096]{1,0:T(8,128)} %param.4) | data formatting | bytes 12582912
  15.4 8.6 %all-to-all-start = ((s32[32,1,4]{2,1,0:T(1,128)}), s32[32,1,4]{2,1,0:T(1,128)S(1)}, u32[]{:S(2)}, u32[]{:S(2)}) async-start(s32[32,1,4]{2,1,0:T(1,128)} %bitcast.4), calls=%async_computation | async-start | bytes 32768 | tf_op jit(solution)/shard_map/all_to_all | solution.py:52
  30.9 5.0 %all-to-all-start.1 = ((f32[32,4,4096]{2,1,0:T(4,128)}), f32[32,4,4096]{2,1,0:T(4,128)}, u32[]{:S(2)}, u32[]{:S(2)}) async-start(f32[32,4,4096]{2,1,0:T(4,128)} %reshape.85), calls=%async_computation.1 | async-start | bytes 4194304 | tf_op jit(solution)/shard_map/all_to_all | solution.py:45
  37.2 27.1 %all-to-all-done.1 = f32[32,4,4096]{2,1,0:T(4,128)} async-done(((f32[32,4,4096]{2,1,0:T(4,128)}), f32[32,4,4096]{2,1,0:T(4,128)}, u32[]{:S(2)}, u32[]{:S(2)}) %all-to-all-start.1) | async-done | bytes 2097184 | tf_op jit(solution)/shard_map/all_to_all | solution.py:45
  66.3 8.7 %scatter_fusion = f32[384,4096]{1,0:T(8,128)} fusion(f32[384,4096]{1,0:T(8,128)} %copy.33, s32[128]{0:T(128)S(1)} %fusion.40, f32[128,4096]{1,0:T(8,128)S(1)} %reshape.126), kind=kCustom, calls=%fused_computation.2 | custom fusion | flops 524288 | bytes 6291968 | tf_op jit(solution)/shard_map/scatter-add | solution.py:56
  76.2 5.7 %collective-permute-start = (f32[384,512]{1,0:T(8,128)S(1)}, f32[384,512]{1,0:T(8,128)S(1)}, u32[]{:S(2)}, u32[]{:S(2)}) collective-permute-start(f32[384,512]{1,0:T(8,128)S(1)} %slice.122), channel_id=1, source_target_pairs={{0,3},{4,7},{8,11},{12,15},{16,19},{20,23},{24,27},{28,31},{32,35}... | collective-permute-start | bytes 2359304 | tf_op jit(solution)/shard_map/ppermute | solution.py:24
  84.8 13.1 %collective-permute-done = f32[384,512]{1,0:T(8,128)S(1)} collective-permute-done((f32[384,512]{1,0:T(8,128)S(1)}, f32[384,512]{1,0:T(8,128)S(1)}, u32[]{:S(2)}, u32[]{:S(2)}) %collective-permute-start) | collective-permute-done | bytes 786464 | tf_op jit(solution)/shard_map/ppermute | solution.py:24
  99.2 16.9 %collective-permute-done.2 = f32[384,512]{1,0:T(8,128)S(1)} collective-permute-done((f32[384,512]{1,0:T(8,128)S(1)}, f32[384,512]{1,0:T(8,128)S(1)}, u32[]{:S(2)}, u32[]{:S(2)}) %collective-permute-start.2) | collective-permute-done | bytes 786464 | tf_op jit(solution)/shard_map/ppermute | solution.py:24
  117.6 17.5 %fusion.48 = f32[512,4096]{0,1:T(8,128)} fusion(f32[384,512]{1,0:T(8,128)S(1)} %select_select_fusion.2, f32[384,4096]{1,0:T(8,128)} %scatter_fusion), kind=kOutput, calls=%fused_computation.95 | convolution fusion | flops 9663676416 | bytes 15466496 | tf_op jit(solution)/shard_map/dot_general | solution.py:14
  135.1 117.8 %all-reduce.3.cloned.1.call-done = f32[512,4096]{0,1:T(8,128)} async-done(((f32[512,4096]{0,1:T(8,128)}), f32[512,4096]{0,1:T(8,128)}) %all-reduce.3.cloned.1.call-update) | async-done | bytes 8388624 | tf_op jit(solution)/shard_map/psum | solution.py:60
  254.2 4.6 collective-permute-start.3
  265.1 15.4 %collective-permute-done.3 = f32[512,512]{0,1:T(8,128)S(1)} collective-permute-done((f32[512,512]{0,1:T(8,128)S(1)}, f32[512,512]{0,1:T(8,128)S(1)}, u32[]{:S(2)}, u32[]{:S(2)}) %collective-permute-start.3) | collective-permute-done | bytes 1048608 | tf_op jit(solution)/shard_map/ppermute | solution.py:24
  281.8 22.5 %collective-permute-done.5 = f32[512,512]{0,1:T(8,128)} collective-permute-done((f32[512,512]{0,1:T(8,128)S(1)}, f32[512,512]{0,1:T(8,128)}, u32[]{:S(2)}, u32[]{:S(2)}) %collective-permute-start.5) | collective-permute-done | bytes 1048608 | tf_op jit(solution)/shard_map/ppermute | solution.py:24
  307.6 11.7 %cholesky.106 = f32[128,128]{1,0:T(8,128)S(1)} custom-call(f32[128,128]{1,0:T(8,128)S(1)} %cholesky.269), custom_call_target="Cholesky" | custom-call | tf_op jit(solution)/shard_map/jit(cholesky)/cholesky | solution.py:62
  319.4 9.8 %custom-call.30 = f32[1,128,128]{1,2,0:T(8,128)S(1)} custom-call(f32[1,128,128]{2,1,0:T(8,128)S(1)} %get-tuple-element.30), custom_call_target="InvertDiagBlocksLowerTriangular" | custom-call | tf_op jit(solution)/shard_map/jit(cholesky)/cholesky | solution.py:62
  331.8 11.7 %cholesky.220 = f32[128,128]{1,0:T(8,128)S(1)} custom-call(f32[128,128]{1,0:T(8,128)S(1)} %cholesky.273), custom_call_target="Cholesky" | custom-call | tf_op jit(solution)/shard_map/jit(cholesky)/cholesky | solution.py:62
  343.5 10.0 %custom-call.31 = f32[1,128,128]{1,2,0:T(8,128)S(1)} custom-call(f32[1,128,128]{2,1,0:T(8,128)S(1)} %get-tuple-element.27), custom_call_target="InvertDiagBlocksLowerTriangular" | custom-call | tf_op jit(solution)/shard_map/jit(cholesky)/cholesky | solution.py:62
  355.1 11.7 %cholesky.241 = f32[128,128]{1,0:T(8,128)S(1)} custom-call(f32[128,128]{1,0:T(8,128)S(1)} %cholesky.278), custom_call_target="Cholesky" | custom-call | tf_op jit(solution)/shard_map/jit(cholesky)/cholesky | solution.py:62
  366.8 9.8 %custom-call.32 = f32[1,128,128]{1,2,0:T(8,128)S(1)} custom-call(f32[1,128,128]{2,1,0:T(8,128)S(1)} %get-tuple-element.24), custom_call_target="InvertDiagBlocksLowerTriangular" | custom-call | tf_op jit(solution)/shard_map/jit(cholesky)/cholesky | solution.py:62
  378.1 11.9 %cholesky.258 = f32[128,128]{1,0:T(8,128)S(1)} custom-call(f32[128,128]{1,0:T(8,128)S(1)} %slice_subtract_fusion.2), custom_call_target="Cholesky" | custom-call | tf_op jit(solution)/shard_map/jit(cholesky)/cholesky | solution.py:62
  395.8 14.3 %while.1 = (s32[]{:T(128)}, f32[512,512]{1,0:T(8,128)}, s32[4,2]{0,1:T(2,128)S(1)}, f32[4,128,128]{2,1,0:T(8,128)}, s32[]{:T(128)}) while((s32[]{:T(128)}, f32[512,512]{1,0:T(8,128)}, s32[4,2]{0,1:T(2,128)S(1)}, f32[4,128,128]{2,1,0:T(8,128)}, s32[]{:T(128)}) %tuple.32), condition=%wide.while_cond, body=%wide.while_body.sunk | while | flops 2 | bytes 132205 | solution.py:63
  410.1 40.1 %custom-call.33 = f32[4,128,128]{1,2,0:T(8,128)S(1)} custom-call(f32[4,128,128]{2,1,0:T(8,128)} %get-tuple-element.10), custom_call_target="InvertDiagBlocksLowerTriangular" | custom-call | tf_op jit(solution)/shard_map/triangular_solve | solution.py:63
  458.3 16.6 %fusion.9 = f32[512,4096]{1,0:T(8,128)S(1)} fusion(f32[512,4096]{0,1:T(8,128)} %all-reduce.3.cloned.1.call-done, f32[128,512]{1,0:T(8,128)S(1)} %fusion.26, f32[128,512]{1,0:T(8,128)S(1)} %fusion.27, f32[128,512]{1,0:T(8,128)S(1)} %fusion.29, f32[128,512]{1,0:T(8,128)S(1)} %fusion.16), kind=kOutput, calls=%fused_computation.27 | convolution fusion | flops 12885688320 | bytes 17825792 | tf_op jit(solution)/shard_map/dot_general | solution.py:14
  475.0 12.4 %convolution_subtract_fusion = f32[384,4096]{1,0:T(8,128)} fusion(f32[384,4096]{1,0:T(8,128)S(1)} %bitcast.66, f32[384,512]{1,0:T(8,128)S(1)} %get-tuple-element.34, f32[512,4096]{1,0:T(8,128)S(1)} %fusion.9), kind=kOutput, calls=%fused_computation.5 | convolution fusion | flops 9665249280 | bytes 21757952 | tf_op jit(solution)/shard_map/dot_general | solution.py:14
  (84 shorter events, 62.5 us)
Async XLA Ops:
  7.2 6.2 %copy-start.3 = (s32[64,1]{0,1:T(1,128)S(1)}, s32[64,1]{0,1:T(1,128)}, u32[]{:S(2)}) copy-start(s32[64,1]{0,1:T(1,128)} %param.6) | copy-start | bytes 772
  15.4 15.5 %all-to-all-start = ((s32[32,1,4]{2,1,0:T(1,128)}), s32[32,1,4]{2,1,0:T(1,128)S(1)}, u32[]{:S(2)}, u32[]{:S(2)}) async-start(s32[32,1,4]{2,1,0:T(1,128)} %bitcast.4), calls=%async_computation | async-start | bytes 32768 | tf_op jit(solution)/shard_map/all_to_all | solution.py:52
  30.9 33.5 %all-to-all-start.1 = ((f32[32,4,4096]{2,1,0:T(4,128)}), f32[32,4,4096]{2,1,0:T(4,128)}, u32[]{:S(2)}, u32[]{:S(2)}) async-start(f32[32,4,4096]{2,1,0:T(4,128)} %reshape.85), calls=%async_computation.1 | async-start | bytes 4194304 | tf_op jit(solution)/shard_map/all_to_all | solution.py:45
  35.9 217.0 %all-reduce.3.cloned.1.call-start = ((), (), s32[]{:S(2)}) async-start(), calls=%async_computation.2 | async-start | bytes 16777216 | tf_op jit(solution)/shard_map/psum | solution.py:60
  76.2 21.7 %collective-permute-start = (f32[384,512]{1,0:T(8,128)S(1)}, f32[384,512]{1,0:T(8,128)S(1)}, u32[]{:S(2)}, u32[]{:S(2)}) collective-permute-start(f32[384,512]{1,0:T(8,128)S(1)} %slice.122), channel_id=1, source_target_pairs={{0,3},{4,7},{8,11},{12,15},{16,19},{20,23},{24,27},{28,31},{32,35}... | collective-permute-start | bytes 2359304 | tf_op jit(solution)/shard_map/ppermute | solution.py:24
  81.9 17.4 %collective-permute-start.1 = (f32[384,512]{1,0:T(8,128)S(1)}, f32[384,512]{1,0:T(8,128)S(1)}, u32[]{:S(2)}, u32[]{:S(2)}) collective-permute-start(f32[384,512]{1,0:T(8,128)S(1)} %slice.122), channel_id=1, source_target_pairs={{0,2},{4,6},{8,10},{12,14},{16,18},{20,22},{24,26},{28,30},{32,34}... | collective-permute-start | bytes 2359304 | tf_op jit(solution)/shard_map/ppermute | solution.py:24
  83.2 32.9 %collective-permute-start.2 = (f32[384,512]{1,0:T(8,128)S(1)}, f32[384,512]{1,0:T(8,128)S(1)}, u32[]{:S(2)}, u32[]{:S(2)}) collective-permute-start(f32[384,512]{1,0:T(8,128)S(1)} %slice.122), channel_id=1, source_target_pairs={{0,1},{4,5},{8,9},{12,13},{16,17},{20,21},{24,25},{28,29},{32,33},... | collective-permute-start | bytes 2359304 | tf_op jit(solution)/shard_map/ppermute | solution.py:24
  254.2 26.3 %collective-permute-start.3 = (f32[512,512]{0,1:T(8,128)S(1)}, f32[512,512]{0,1:T(8,128)S(1)}, u32[]{:S(2)}, u32[]{:S(2)}) collective-permute-start(f32[512,512]{0,1:T(8,128)S(1)} %slice.123), channel_id=1, source_target_pairs={{0,3},{4,7},{8,11},{12,15},{16,19},{20,23},{24,27},{28,31},{32,35}... | collective-permute-start | bytes 3145736 | tf_op jit(solution)/shard_map/ppermute | solution.py:24
  258.8 23.0 %collective-permute-start.4 = (f32[512,512]{0,1:T(8,128)S(1)}, f32[512,512]{0,1:T(8,128)}, u32[]{:S(2)}, u32[]{:S(2)}) collective-permute-start(f32[512,512]{0,1:T(8,128)S(1)} %slice.123), channel_id=1, source_target_pairs={{0,2},{4,6},{8,10},{12,14},{16,18},{20,22},{24,26},{28,30},{32,34}... | collective-permute-start | bytes 3145736 | tf_op jit(solution)/shard_map/ppermute | solution.py:24
  261.1 43.2 %collective-permute-start.5 = (f32[512,512]{0,1:T(8,128)S(1)}, f32[512,512]{0,1:T(8,128)}, u32[]{:S(2)}, u32[]{:S(2)}) collective-permute-start(f32[512,512]{0,1:T(8,128)S(1)} %slice.123), channel_id=1, source_target_pairs={{0,1},{4,5},{8,9},{12,13},{16,17},{20,21},{24,25},{28,29},{32,33},... | collective-permute-start | bytes 3145736 | tf_op jit(solution)/shard_map/ppermute | solution.py:24
  306.6 1.0 copy-start.2
  307.5 143.0 %copy-start.1 = (f32[512,512]{1,0:T(8,128)S(1)}, f32[512,512]{1,0:T(8,128)}, u32[]{:S(2)}) copy-start(f32[512,512]{1,0:T(8,128)} %fusion.13) | copy-start | bytes 3145732
  456.0 19.0 %slice-start = ((s8[6291456]{0:T(1024)(128)(4,1)}), s8[4194304]{0:T(1024)(128)(4,1)S(1)}, s32[]{:S(2)}) async-start(s8[6291456]{0:T(1024)(128)(4,1)} %bitcast.65), calls=%async_computation.3 | async-start | bytes 8388608
  458.3 16.7 %slice-start.1 = ((s8[6291456]{0:T(1024)(128)(4,1)}), s8[2097152]{0:T(1024)(128)(4,1)S(1)}, s32[]{:S(2)}) async-start(s8[6291456]{0:T(1024)(128)(4,1)} %bitcast.65), calls=%async_computation.4 | async-start | bytes 4194304
  475.0 12.5 %copy-start = (f32[512,4096]{1,0:T(8,128)}, f32[512,4096]{1,0:T(8,128)S(1)}, u32[]{:S(2)}) copy-start(f32[512,4096]{1,0:T(8,128)S(1)} %fusion.9) | copy-start | bytes 25165828
Sparse Core Ops, SparseCore 0:
  135.2 117.6 all-reduce.2

commit v2 on v1

--- a/solution.py
+++ b/solution.py
@@ -1,19 +1,387 @@
+import functools
 import math
 
 import jax
 import jax.numpy as jnp
 from jax import lax
+from jax.experimental import pallas as pl
+from jax.experimental.pallas import tpu as pltpu
 from jax.sharding import PartitionSpec as P
 
 PB = 128
 PANELS = 4
 WIDE = PB * PANELS
+MESH = pl.DeviceIdType.MESH
+F32 = jnp.float32
+BF16 = jnp.bfloat16
+SIDE = 4
+HALF = WIDE // 2
+SHARD = HALF // SIDE
+SUB = SHARD // SIDE
+CW = 1024
+COPIES = 22
 
 
 def product(left_op, right_op):
     return jnp.dot(
-        left_op, right_op, precision=lax.Precision.HIGHEST, preferred_element_type=jnp.float32
-    )
+        left_op, right_op, precision=lax.Precision.HIGHEST, preferred_element_type=F32
+    )
+
+
+def split(value):
+    high = value.astype(BF16)
+    return high, (value - high.astype(F32)).astype(BF16)
+
+
+def dot3(lh, ll, rh, rl):
+    def one(a, b):
+        return jnp.dot(a, b, preferred_element_type=F32)
+
+    return one(lh, rh) + (one(lh, rl) + one(ll, rh))
+
+
+def chol_steps(dblk, xblk, start, stop):
+    lane = lax.broadcasted_iota(jnp.int32, (PB, PB), 1)
+    sub = lax.broadcasted_iota(jnp.int32, (PB, PB), 0)
+
+    def step(j, carry):
+        a = dblk[...]
+        x = xblk[...]
+        row = dblk[pl.ds(j, 1), :]
+        xrow = xblk[pl.ds(j, 1), :]
+        col = jnp.sum(jnp.where(lane == j, a, 0.0), axis=1, keepdims=True)
+        piv = jnp.sum(
+            jnp.where(lax.broadcasted_iota(jnp.int32, (1, PB), 1) == j, row, 0.0),
+            axis=1,
+            keepdims=True,
+        )
+        inv = 1.0 / jnp.sqrt(piv)
+        below = sub > j
+        here = sub == j
+        mult = col * (inv * inv)
+        dblk[...] = jnp.where(below, a - mult * row, a)
+        xblk[...] = jnp.where(below, x - mult * xrow, jnp.where(here, x * inv, x))
+        return carry
+
+    lax.fori_loop(start, stop, step, 0)
+
+
+def tdot(a, b):
+    return lax.dot_general(
+        a, b, (((1,), (1,)), ((), ())), precision=lax.Precision.HIGHEST, preferred_element_type=F32
+    )
+
+
+def main_kernel(
+    a1_ref, a1t_ref, w_ref, f_ref, linv_ref,
+    p_ref, ah, al, r0, r1, r2, g_ref, dblk, xblk, lcol,
+    send_sem, recv_sem,
+):
+    r = lax.axis_index("row")
+    core = lax.rem(r, 2)
+    yy = lax.rem(r // 2, SIDE)
+    xx = r // (2 * SIDE)
+    other = 1 - core
+    a = other * xx + core * yy
+    b = core * xx + other * yy
+
+    def at(first, second):
+        px = other * first + core * second
+        py = core * first + other * second
+        return (px * SIDE + py) * 2 + core
+
+    a_up, a_dn, a_op = lax.rem(a + 1, SIDE), lax.rem(a + 3, SIDE), lax.rem(a + 2, SIDE)
+    b_up, b_dn, b_op = lax.rem(b + 1, SIDE), lax.rem(b + 3, SIDE), lax.rem(b + 2, SIDE)
+    partner = r + 1 - 2 * core
+    dev = {
+        "p": partner,
+        "a+": at(a_up, b),
+        "a-": at(a_dn, b),
+        "b+": at(a, b_up),
+        "b-": at(a, b_dn),
+    }
+    barrier = pltpu.get_barrier_semaphore()
+    for peer in dev.values():
+        pl.semaphore_signal(barrier, inc=1, device_id={"row": peer}, device_id_type=MESH)
+    pl.semaphore_wait(barrier, len(dev))
+
+    total_cols = w_ref.shape[1]
+    chunks = [(0, WIDE)] + [(WIDE + i * CW, CW) for i in range(total_cols // CW)]
+    n = len(chunks)
+    started = {}
+
+    def send(c, slot, src, dst, where):
+        copy = pltpu.make_async_remote_copy(
+            src_ref=src,
+            dst_ref=dst,
+            send_sem=send_sem.at[c, slot],
+            recv_sem=recv_sem.at[c, slot],
+            device_id={"row": dev[where]},
+            device_id_type=MESH,
+        )
+        copy.start()
+        started[(c, slot)] = copy
+
+    def got(c, slot):
+        started[(c, slot)].wait_recv()
+
+    own = HALF * core
+
+    def mult8(v, m=8):
+        return pl.multiple_of(v, m)
+
+    def shard(i, half=0):
+        return mult8(own + SHARD * i + half * (SHARD // 2))
+
+    def sub(i, half=0):
+        return mult8(own + SHARD * a + SUB * i + half * (SUB // 2))
+
+    def fill(c):
+        c0, cw = chunks[c]
+        if c == 0:
+            p_ref[:, pl.ds(0, WIDE)] = product(a1t_ref[...], a1_ref[...])
+            hi, lo = split(a1t_ref[...])
+            ah[...] = hi
+            al[...] = lo
+            return
+
+        def tile(i, carry):
+            off = pl.multiple_of(c0 - WIDE + i * 256, 256)
+            wh, wl = split(w_ref[:, pl.ds(off, 256)])
+            p_ref[:, pl.ds(pl.multiple_of(off + WIDE, 256), 256)] = dot3(ah[...], al[...], wh, wl)
+            return carry
+
+        lax.fori_loop(0, cw // 256, tile, 0)
+
+    def phase(c, p):
+        c0, cw = chunks[c]
+        cols = pl.ds(c0, cw)
+
+        def part(row, count):
+            return p_ref.at[pl.ds(row, count), cols]
+
+        def full(row, count):
+            return f_ref.at[pl.ds(row, count), cols]
+
+        def add(row, count, *sources):
+            rows = pl.ds(row, count)
+            value = p_ref[rows, cols]
+            for source in sources:
+                value = value + source[...]
+            p_ref[rows, cols] = value
+
+        s32, s8 = SHARD // 2, SUB // 2
+        one = lambda i: r1.at[pl.ds(i * s32, s32), cols]
+        two = lambda i: r2.at[pl.ds(i * s8, s8), cols]
+        if p == 0:
+            fill(c)
+            there = mult8(HALF * other)
+            send(c, 0, part(there, HALF), r0.at[:, cols], "p")
+        elif p == 1:
+            got(c, 0)
+            add(mult8(own), HALF, r0.at[:, cols])
+            send(c, 1, part(shard(a_op, 0), s32), one(0), "a+")
+            send(c, 2, part(shard(a_op, 1), s32), one(1), "a-")
+            send(c, 3, part(shard(a_up, 1), s32), one(2), "a+")
+            send(c, 4, part(shard(a_dn, 0), s32), one(3), "a-")
+        elif p == 2:
+            got(c, 1)
+            add(shard(a_up, 0), s32, one(0))
+            send(c, 5, part(shard(a_up, 0), s32), one(4), "a+")
+            got(c, 2)
+            add(shard(a_dn, 1), s32, one(1))
+            send(c, 6, part(shard(a_dn, 1), s32), one(5), "a-")
+        elif p == 3:
+            for slot in (3, 4, 5, 6):
+                got(c, slot)
+            add(shard(a, 0), s32, one(3), one(4))
+            add(shard(a, 1), s32, one(2), one(5))
+            send(c, 7, part(sub(b_op, 0), s8), two(0), "b+")
+            send(c, 8, part(sub(b_op, 1), s8), two(1), "b-")
+            send(c, 9, part(sub(b_up, 1), s8), two(2), "b+")
+            send(c, 10, part(sub(b_dn, 0), s8), two(3), "b-")
+        elif p == 4:
+            got(c, 7)
+            add(sub(b_up, 0), s8, two(0))
+            send(c, 11, part(sub(b_up, 0), s8), two(4), "b+")
+            got(c, 8)
+            add(sub(b_dn, 1), s8, two(1))
+            send(c, 12, part(sub(b_dn, 1), s8), two(5), "b-")
+        elif p == 5:
+            for slot in (9, 10, 11, 12):
+                got(c, slot)
+            f_ref[pl.ds(sub(b, 0), s8), cols] = (
+                p_ref[pl.ds(sub(b, 0), s8), cols] + two(3)[...] + two(4)[...]
+            )
+            f_ref[pl.ds(sub(b, 1), s8), cols] = (
+                p_ref[pl.ds(sub(b, 1), s8), cols] + two(2)[...] + two(5)[...]
+            )
+            send(c, 13, full(sub(b), SUB), full(sub(b), SUB), "b+")
+            send(c, 14, full(sub(b), SUB), full(sub(b), SUB), "b-")
+        elif p == 6:
+            got(c, 13)
+            send(c, 15, full(sub(b_dn, 0), s8), full(sub(b_dn, 0), s8), "b+")
+            got(c, 14)
+            send(c, 16, full(sub(b_up, 1), s8), full(sub(b_up, 1), s8), "b-")
+        elif p == 7:
+            got(c, 15)
+            got(c, 16)
+            send(c, 17, full(shard(a), SHARD), full(shard(a), SHARD), "a+")
+            send(c, 18, full(shard(a), SHARD), full(shard(a), SHARD), "a-")
+        elif p == 8:
+            got(c, 17)
+            send(c, 19, full(shard(a_dn, 0), s32), full(shard(a_dn, 0), s32), "a+")
+            got(c, 18)
+            send(c, 20, full(shard(a_up, 1), s32), full(shard(a_up, 1), s32), "a-")
+        elif p == 9:
+            got(c, 19)
+            got(c, 20)
+            send(c, 21, full(mult8(own), HALF), full(mult8(own), HALF), "p")
+        elif p == 10:
+            got(c, 21)
+
+    def chol_begin(k):
+        if k == 0:
+            g_ref[...] = f_ref[:, pl.ds(0, WIDE)]
+            linv_ref[...] = jnp.zeros_like(linv_ref)
+        d = pl.ds(k * PB, PB)
+        dblk[...] = g_ref[d, d]
+        xblk[...] = jnp.where(
+            lax.broadcasted_iota(jnp.int32, (PB, PB), 0)
+            == lax.broadcasted_iota(jnp.int32, (PB, PB), 1),
+            1.0,
+            0.0,
+        ).astype(F32)
+
+    def chol_end(k):
+        d = pl.ds(k * PB, PB)
+        x = xblk[...]
+        if k:
+            left = pl.ds(0, k * PB)
+            linv_ref[d, left] = -product(x, product(g_ref[d, left], linv_ref[left, left]))
+        linv_ref[d, d] = x
+        if k < PANELS - 1:
+            rest = pl.ds((k + 1) * PB, (PANELS - 1 - k) * PB)
+            below = tdot(g_ref[rest, d], x)
+            g_ref[rest, d] = below
+            g_ref[rest, rest] = g_ref[rest, rest] - tdot(below, below)
+
+    pieces = []
+    for k in range(PANELS):
+        for q in range(2):
+            pieces.append((k, q))
+
+    def piece(k, q):
+        if q == 0:
+            chol_begin(k)
+        chol_steps(dblk, xblk, q * (PB // 2), (q + 1) * (PB // 2))
+        if q == 1:
+            chol_end(k)
+
+    last = 2 * (n - 1) + 10
+    nxt = 0
+    for t in range(last + 1):
+        for c in range(n):
+            p = t - 2 * c
+            if 0 <= p <= 10:
+                phase(c, p)
+        if t >= 10 and nxt < len(pieces):
+            piece(*pieces[nxt])
+            nxt += 1
+    while nxt < len(pieces):
+        piece(*pieces[nxt])
+        nxt += 1
+    for copy in started.values():
+        copy.wait_send()
+
+
+def all_reduced(a1, a1t, w):
+    rows, cols = w.shape
+    wide = cols + WIDE
+    n = 1 + cols // CW
+    vm = pl.BlockSpec(memory_space=pltpu.VMEM)
+    return pl.pallas_call(
+        main_kernel,
+        out_shape=(
+            jax.ShapeDtypeStruct((WIDE, wide), F32),
+            jax.ShapeDtypeStruct((WIDE, WIDE), F32),
+        ),
+        in_specs=[vm] * 3,
+        out_specs=(vm, vm),
+        scratch_shapes=[
+            pltpu.VMEM((WIDE, wide), F32),
+            pltpu.VMEM((WIDE, rows), BF16),
+            pltpu.VMEM((WIDE, rows), BF16),
+            pltpu.VMEM((HALF, wide), F32),
+            pltpu.VMEM((6 * SHARD // 2, wide), F32),
+            pltpu.VMEM((6 * SUB // 2, wide), F32),
+            pltpu.VMEM((WIDE, WIDE), F32),
+            pltpu.VMEM((PB, PB), F32),
+            pltpu.VMEM((PB, PB), F32),
+            pltpu.VMEM((PB, PB), F32),
+            pltpu.SemaphoreType.DMA((n, COPIES)),
+            pltpu.SemaphoreType.DMA((n, COPIES)),
+        ],
+        compiler_params=pltpu.CompilerParams(
+            collective_id=0, has_side_effects=True, vmem_limit_bytes=60 * 1024 * 1024
+        ),
+        name="all_reduce_gram",
+    )(a1, a1t, w)
+
+
+def tail_kernel(scale, a1_ref, linv_ref, s_ref, w_ref, u_ref, o_ref, q_ref, lh, ll, qh, ql):
+    @pl.when(pl.program_id(0) == 0)
+    def _():
+        linv = linv_ref[...]
+        hi, lo = split(linv)
+        lh[...] = hi
+        ll[...] = lo
+        basis = tdot(a1_ref[...], linv)
+        q_ref[...] = basis * scale
+        hi, lo = split(basis)
+        qh[...] = hi
+        ql[...] = lo
+
+    sh, sl = split(s_ref[...])
+    u = dot3(lh[...], ll[...], sh, sl)
+    u_ref[...] = u
+    uh, ul = split(u)
+    o_ref[...] = w_ref[...] - dot3(qh[...], ql[...], uh, ul)
+
+
+def tail(a1, linv, sums, w, scale):
+    rows, cols = w.shape
+    tc = 512
+    off = WIDE // tc
+    whole = lambda shape: pl.BlockSpec(shape, lambda i: (0, 0))
+    return pl.pallas_call(
+        functools.partial(tail_kernel, scale),
+        grid=(cols // tc,),
+        out_shape=(
+            jax.ShapeDtypeStruct((WIDE, cols), F32),
+            jax.ShapeDtypeStruct((rows, cols), F32),
+            jax.ShapeDtypeStruct((rows, WIDE), F32),
+        ),
+        in_specs=[
+            whole((rows, WIDE)),
+            whole((WIDE, WIDE)),
+            pl.BlockSpec((WIDE, tc), lambda i: (0, i + off)),
+            pl.BlockSpec((rows, tc), lambda i: (0, i)),
+        ],
+        out_specs=(
+            pl.BlockSpec((WIDE, tc), lambda i: (0, i)),
+            pl.BlockSpec((rows, tc), lambda i: (0, i)),
+            whole((rows, WIDE)),
+        ),
+        scratch_shapes=[
+            pltpu.VMEM((WIDE, WIDE), BF16),
+            pltpu.VMEM((WIDE, WIDE), BF16),
+            pltpu.VMEM((rows, WIDE), BF16),
+            pltpu.VMEM((rows, WIDE), BF16),
+        ],
+        compiler_params=pltpu.CompilerParams(vmem_limit_bytes=40 * 1024 * 1024),
+        name="project_out",
+    )(a1, linv, sums, w)
 
 
 def from_first(block, axis):
@@ -57,17 +425,8 @@
         received.reshape(slot_total, local_cols), mode="drop"
     )
     panel = from_first(current[:, :WIDE], "col")
-    inner = lax.psum(product(panel.T, current), "row")
-    gram = from_first(inner[:, :WIDE], "col")
-    lower_factor = jnp.linalg.cholesky(gram)
-    inverse = lax.linalg.triangular_solve(
-        lower_factor, jnp.eye(WIDE, dtype=jnp.float32), left_side=True, lower=True
-    )
-    upper = product(inverse, inner)
-    basis = product(panel, inverse.T)
-    reduced = current - product(basis, upper)
-    total_rows = local_rows * row_count
-    return (upper, reduced, basis * math.sqrt(total_rows))
+    sums, linv = all_reduced(panel, panel.T, current)
+    return tail(panel, linv, sums, current, math.sqrt(local_rows * row_count))
 
 
 def solution(mesh):

time: 502 us -> 257 us (0.51); the launches traced: 495 us -> 256 us
  waiting for transfers between devices: 218 us -> 58.9 us
  Pallas kernels: 0 us -> 142 us
  other arithmetic: 134 us -> 11.2 us
  matrix products: 60 us -> 0 us
  between operations: 17.4 us -> 0.78 us
  local copies, waits for them, and re-layouts: 32.7 us -> 21.9 us
  starting transfers between devices: 31.8 us -> 21.2 us
    pallas_call x0 -> x2, Pallas kernels: none -> 142 us  [the longest x1 125 us: all_reduced(): pl.pallas_call(main_kernel, out_shape=(jax.ShapeDtypeStruct((WIDE, wide),...]
    another operation x17 -> x0, other arithmetic: 120 us -> none  [the longest x14 78.8 us: on_device(): lower_factor = jnp.linalg.cholesky(gram)]
    psum x1 -> x0, waiting for transfers between devices: 118 us -> none  [on_device(): inner = lax.psum(product(panel.T, current), 'row')]
    dot_general x4 -> x0, matrix products: 48.9 us -> none  [product(): jnp.dot(left_op, right_op, precision=lax.Precision.HIGHEST, preferred_ele...]
    ppermute x6 -> x3, waiting for transfers between devices: 70.5 us -> 28.8 us  [from_first(): got = lax.ppermute(block, axis, [(0, peer)])]
    another operation x17 -> x0, local copies, waits for them, and re-layouts: 14.5 us -> none
    another operation x13 -> x0, matrix products: 11.1 us -> none  [the longest x7 5.67 us: on_device(): lax.linalg.triangular_solve(lower_factor, jnp.eye(WIDE, dtype=jnp.float32...]
    ppermute x6 -> x3, starting transfers between devices: 18.2 us -> 7.6 us  [from_first(): got = lax.ppermute(block, axis, [(0, peer)])]
  transfers between devices with their start and end apart: 9 -> 5, of which waited for: 9 -> 4; matrix products, arithmetic and copies ran while one was open for 1% -> 2% of each run, Pallas kernels for 0% -> 0%
where the time goes in v2:
time: 257 us; the launch traced here: 256 us
  Pallas kernels  142 us (55%)
  waiting for transfers between devices  58.9 us (23%)
  local copies, waits for them, and re-layouts  21.9 us (9%)
  starting transfers between devices  21.2 us (8%)
  other arithmetic  11.2 us (4%)
    pallas_call x1, Pallas kernels, all_reduced(): pl.pallas_call(main_kernel, out_shape=(jax.ShapeDtypeStruct((WIDE, wide),...  125 us
    ppermute x3, waiting for transfers between devices, from_first(): got = lax.ppermute(block, axis, [(0, peer)])  28.8 us
    all_to_all x1, waiting for transfers between devices, on_device(): lax.all_to_all(sender.reshape(row_count, capacity, local_cols), 'row', sp...  27.2 us
    pallas_call x1, Pallas kernels, tail(): pl.pallas_call(functools.partial(tail_kernel, scale), grid=(cols // tc,),...  17.7 us
    unnamed x11, local copies, waits for them, and re-layouts  11.3 us
    scatter-add x1, other arithmetic, on_device(): front_matrix.at[placed.reshape(slot_total)]  8.66 us
    all_to_all x1, starting transfers between devices, on_device(): lax.all_to_all(offsets.reshape(row_count, capacity), 'row', split_axis=0,...  8.58 us
    ppermute x3, starting transfers between devices, from_first(): got = lax.ppermute(block, axis, [(0, peer)])  7.6 us
  transfers between devices with their start and end apart: 5, of which 4 were waited for; matrix products, arithmetic and copies ran while one was open for 2% of the time, Pallas kernels for 0%

profile of v2, /device:TPU:1, one launch (start us, length us, event | category | flops | bytes accessed | tf_op | source)
XLA Modules:
  0.0 256.2 jit_solution(14059566394621600147)
XLA Ops:
  0.6 6.2 %copy.13 = f32[384,4096]{1,0:T(8,128)} copy(f32[384,4096]{1,0:T(8,128)} %param.4) | data formatting | bytes 12582912
  7.2 0.9 scatter_custom_fusion
  8.1 0.7 all_to_all.9
  8.8 8.6 %all-to-all-start = ((s32[32,1,4]{2,1,0:T(1,128)}), s32[32,1,4]{2,1,0:T(1,128)S(1)}, u32[]{:S(2)}, u32[]{:S(2)}) async-start(s32[32,1,4]{2,1,0:T(1,128)} %bitcast.4), calls=%async_computation | async-start | bytes 32768 | tf_op jit(solution)/shard_map/all_to_all | solution.py:420
  17.4 2.4 scatter_custom_fusion.1
  19.8 1.6 reshape.50
  21.4 2.9 %all-to-all-done = s32[32,1,4]{2,1,0:T(1,128)S(1)} async-done(((s32[32,1,4]{2,1,0:T(1,128)}), s32[32,1,4]{2,1,0:T(1,128)S(1)}, u32[]{:S(2)}, u32[]{:S(2)}) %all-to-all-start) | async-done | bytes 544 | tf_op jit(solution)/shard_map/all_to_all | solution.py:420
  24.3 5.0 %all-to-all-start.1 = ((f32[32,4,4096]{2,1,0:T(4,128)}), f32[32,4,4096]{2,1,0:T(4,128)}, u32[]{:S(2)}, u32[]{:S(2)}) async-start(f32[32,4,4096]{2,1,0:T(4,128)} %reshape.50), calls=%async_computation.1 | async-start | bytes 4194304 | tf_op jit(solution)/shard_map/all_to_all | solution.py:413
  30.6 27.2 %all-to-all-done.1 = f32[32,4,4096]{2,1,0:T(4,128)} async-done(((f32[32,4,4096]{2,1,0:T(4,128)}), f32[32,4,4096]{2,1,0:T(4,128)}, u32[]{:S(2)}, u32[]{:S(2)}) %all-to-all-start.1) | async-done | bytes 2097184 | tf_op jit(solution)/shard_map/all_to_all | solution.py:413
  57.8 2.0 reshape.72
  59.8 8.7 %scatter_fusion = f32[384,4096]{1,0:T(8,128)} fusion(f32[384,4096]{1,0:T(8,128)} %copy.13, s32[128]{0:T(128)S(1)} %fusion.4, f32[128,4096]{1,0:T(8,128)S(1)} %reshape.72), kind=kCustom, calls=%fused_computation.2 | custom fusion | flops 524288 | bytes 6291968 | tf_op jit(solution)/shard_map/scatter-add | solution.py:424
  68.4 1.2 slice.4
  69.6 3.6 %collective-permute-start.2 = (f32[384,512]{1,0:T(8,128)S(1)}, f32[384,512]{1,0:T(8,128)S(1)}, u32[]{:S(2)}, u32[]{:S(2)}) collective-permute-start(f32[384,512]{1,0:T(8,128)S(1)} %slice.4), channel_id=1, source_target_pairs={{0,1},{4,5},{8,9},{12,13},{16,17},{20,21},{24,25},{28,29},{32,33},... | collective-permute-start | bytes 2359304 | tf_op jit(solution)/shard_map/ppermute | solution.py:392
  73.2 2.7 %collective-permute-start.1 = (f32[384,512]{1,0:T(8,128)S(1)}, f32[384,512]{1,0:T(8,128)S(1)}, u32[]{:S(2)}, u32[]{:S(2)}) collective-permute-start(f32[384,512]{1,0:T(8,128)S(1)} %slice.4), channel_id=1, source_target_pairs={{0,2},{4,6},{8,10},{12,14},{16,18},{20,22},{24,26},{28,30},{32,34}... | collective-permute-start | bytes 2359304 | tf_op jit(solution)/shard_map/ppermute | solution.py:392
  75.9 1.3 collective-permute-start
  77.3 12.0 %collective-permute-done.2 = f32[384,512]{1,0:T(8,128)S(1)} collective-permute-done((f32[384,512]{1,0:T(8,128)S(1)}, f32[384,512]{1,0:T(8,128)S(1)}, u32[]{:S(2)}, u32[]{:S(2)}) %collective-permute-start.2) | collective-permute-done | bytes 786464 | tf_op jit(solution)/shard_map/ppermute | solution.py:392
  89.2 16.9 %collective-permute-done.1 = f32[384,512]{1,0:T(8,128)S(1)} collective-permute-done((f32[384,512]{1,0:T(8,128)S(1)}, f32[384,512]{1,0:T(8,128)S(1)}, u32[]{:S(2)}, u32[]{:S(2)}) %collective-permute-start.1) | collective-permute-done | bytes 786464 | tf_op jit(solution)/shard_map/ppermute | solution.py:392
  106.1 1.5 select_select_fusion.a1_ref
  107.6 1.1 copy.10.a1t_ref
  108.7 124.7 %all_reduce_gram.1 = (f32[512,4608]{1,0:T(8,128)}, f32[512,512]{1,0:T(8,128)}) custom-call(f32[384,512]{1,0:T(8,128)} %copy-done.1, f32[512,384]{1,0:T(8,128)} %copy.10.a1t_ref, f32[384,4096]{1,0:T(8,128)} %scatter_fusion), custom_call_target="tpu_custom_call" | custom-call | tf_op jit(solution)/shard_map/all_reduce_gram/pallas_call | solution.py:303
  233.4 2.8 %copy-done = f32[384,4096]{1,0:T(8,128)S(1)} copy-done((f32[384,4096]{1,0:T(8,128)S(1)}, f32[384,4096]{1,0:T(8,128)}, u32[]{:S(2)}) %copy-start) | copy-done | bytes 6291480
  236.2 1.1 copy-done.2
  237.3 1.2 copy-done.3
  238.6 17.7 %project_out.1 = (f32[512,4096]{1,0:T(8,128)}, f32[384,4096]{1,0:T(8,128)}, f32[384,512]{1,0:T(8,128)}) custom-call(f32[384,512]{1,0:T(8,128)S(1)} %copy-done.2, f32[512,512]{1,0:T(8,128)S(1)} %copy-done.3, f32[512,4608]{1,0:T(8,128)} %get-tuple-element.6.s_ref, f32[384,4096]{1,0:T(8,128)S(1)} %copy-done), custom_call_target="tpu_custom_call" | custom-call | tf_op jit(solution)/shard_map/project_out/pallas_call | solution.py:357
  (16 shorter events, 1.7 us)
Async XLA Ops:
  0.6 6.2 %copy-start.4 = (s32[64,1]{0,1:T(1,128)S(1)}, s32[64,1]{0,1:T(1,128)}, u32[]{:S(2)}) copy-start(s32[64,1]{0,1:T(1,128)} %param.6) | copy-start | bytes 772
  8.8 15.5 %all-to-all-start = ((s32[32,1,4]{2,1,0:T(1,128)}), s32[32,1,4]{2,1,0:T(1,128)S(1)}, u32[]{:S(2)}, u32[]{:S(2)}) async-start(s32[32,1,4]{2,1,0:T(1,128)} %bitcast.4), calls=%async_computation | async-start | bytes 32768 | tf_op jit(solution)/shard_map/all_to_all | solution.py:420
  24.3 33.5 %all-to-all-start.1 = ((f32[32,4,4096]{2,1,0:T(4,128)}), f32[32,4,4096]{2,1,0:T(4,128)}, u32[]{:S(2)}, u32[]{:S(2)}) async-start(f32[32,4,4096]{2,1,0:T(4,128)} %reshape.50), calls=%async_computation.1 | async-start | bytes 4194304 | tf_op jit(solution)/shard_map/all_to_all | solution.py:413
  69.6 19.6 %collective-permute-start.2 = (f32[384,512]{1,0:T(8,128)S(1)}, f32[384,512]{1,0:T(8,128)S(1)}, u32[]{:S(2)}, u32[]{:S(2)}) collective-permute-start(f32[384,512]{1,0:T(8,128)S(1)} %slice.4), channel_id=1, source_target_pairs={{0,1},{4,5},{8,9},{12,13},{16,17},{20,21},{24,25},{28,29},{32,33},... | collective-permute-start | bytes 2359304 | tf_op jit(solution)/shard_map/ppermute | solution.py:392
  73.2 32.9 %collective-permute-start.1 = (f32[384,512]{1,0:T(8,128)S(1)}, f32[384,512]{1,0:T(8,128)S(1)}, u32[]{:S(2)}, u32[]{:S(2)}) collective-permute-start(f32[384,512]{1,0:T(8,128)S(1)} %slice.4), channel_id=1, source_target_pairs={{0,2},{4,6},{8,10},{12,14},{16,18},{20,22},{24,26},{28,30},{32,34}... | collective-permute-start | bytes 2359304 | tf_op jit(solution)/shard_map/ppermute | solution.py:392
  75.9 30.2 %collective-permute-start = (f32[384,512]{1,0:T(8,128)S(1)}, f32[384,512]{1,0:T(8,128)S(1)}, u32[]{:S(2)}, u32[]{:S(2)}) collective-permute-start(f32[384,512]{1,0:T(8,128)S(1)} %slice.4), channel_id=1, source_target_pairs={{0,3},{4,7},{8,11},{12,15},{16,19},{20,23},{24,27},{28,31},{32,35}... | collective-permute-start | bytes 2359304 | tf_op jit(solution)/shard_map/ppermute | solution.py:392
  107.6 1.2 copy-start.1
  233.4 2.8 %copy-start = (f32[384,4096]{1,0:T(8,128)S(1)}, f32[384,4096]{1,0:T(8,128)}, u32[]{:S(2)}) copy-start(f32[384,4096]{1,0:T(8,128)} %scatter_fusion) | copy-start | bytes 18874372
  236.2 1.1 copy-start.2
  237.3 1.2 copy-start.3

commit v3 on v2

v3 whole, which is shorter than its diff:
```python
import functools
import math

import jax
import jax.numpy as jnp
from jax import lax
from jax.experimental import pallas as pl
from jax.experimental.pallas import tpu as pltpu
from jax.sharding import PartitionSpec as P

PB = 128
PANELS = 4
WIDE = PB * PANELS
MESH = pl.DeviceIdType.MESH
F32 = jnp.float32
BF16 = jnp.bfloat16
SIDE = 4
HALF = WIDE // 2
SHARD = HALF // SIDE
SUB = SHARD // SIDE
CW = 512
HC = 256
TAG = 128
GROUP = 4
GRAM_TAU = (-2, -1, 2, 3, 4, 5, 6)
PIECES = 4
COPIES = 22
ZROWS = 32


def product(left_op, right_op):
    return jnp.dot(
        left_op, right_op, precision=lax.Precision.HIGHEST, preferred_element_type=F32
    )


def split(value):
    high = value.astype(BF16)
    return high, (value - high.astype(F32)).astype(BF16)


def split3(value):
    high = value.astype(BF16)
    rest = value - high.astype(F32)
    mid = rest.astype(BF16)
    return high, mid, (rest - mid.astype(F32)).astype(BF16)


def place(onehot, value):
    high, mid, low = split3(value)

    def one(part):
        return jnp.dot(onehot, part, preferred_element_type=F32)

    return one(high) + (one(mid) + one(low))


def dot3(lh, ll, rh, rl):
    def one(a, b):
        return jnp.dot(a, b, preferred_element_type=F32)

    return one(lh, rh) + (one(lh, rl) + one(ll, rh))


def chol_steps(dblk, xblk, start, stop):
    lane = lax.broadcasted_iota(jnp.int32, (PB, PB), 1)
    lane1 = lax.broadcasted_iota(jnp.int32, (1, PB), 1)
    sub = lax.broadcasted_iota(jnp.int32, (PB, PB), 0)

    def step(i, carry):
        j = i * GROUP
        a, x = dblk[...], xblk[...]
        span = range(GROUP)
        rows = [dblk[pl.ds(j + q, 1), :] for q in span]
        xrows = [xblk[pl.ds(j + q, 1), :] for q in span]
        cols = [
            jnp.sum(jnp.where(lane == j + q, a, 0.0), axis=1, keepdims=True) for q in span
        ]
        m = {
            (p, q): jnp.sum(jnp.where(lane1 == j + q, rows[p], 0.0), axis=1, keepdims=True)
            for p in span
            for q in range(p, GROUP)
        }
        invs = []
        for p in span:
            inv = lax.rsqrt(m[p, p])
            inv2 = inv * inv
            invs.append(inv)
            for q in range(p + 1, GROUP):
                f = m[p, q] * inv2
                rows[q] = rows[q] - f * rows[p]
                xrows[q] = xrows[q] - f * xrows[p]
                cols[q] = cols[q] - f * cols[p]
                for r in range(q, GROUP):
                    m[q, r] = m[q, r] - f * m[p, r]
            cols[p] = cols[p] * inv2
        below = sub > j + GROUP - 1
        na, nx = a, x
        for p in span:
            na = na - cols[p] * rows[p]
            nx = nx - cols[p] * xrows[p]
        nx = jnp.where(below, nx, x)
        for p in span:
            nx = jnp.where(sub == j + p, xrows[p] * invs[p], nx)
        dblk[...] = jnp.where(below, na, a)
        xblk[...] = nx
        return carry

    lax.fori_loop(start // GROUP, stop // GROUP, step, 0)


def tdot(a, b):
    return lax.dot_general(
        a, b, (((1,), (1,)), ((), ())), precision=lax.Precision.HIGHEST, preferred_element_type=F32
    )


def main_kernel(
    child_ref, ocol_ref, orow_ref, off_ref, front_ref,
    w_out, f_out, a1_out, linv_ref,
    w_ref, f_ref, p_ref, a1_ref, ah, al, r0, r1, r2, g_ref, dblk, xblk,
    outbox, inbox, onehot,
    send_sem, recv_sem, box_send, box_recv, z_send, z_recv, local_sem,
):
    count = lax.axis_size("row")
    deep = lax.axis_size("col")
    r = lax.axis_index("row")
    z = lax.axis_index("col")
    core = lax.rem(r, 2)
    yy = lax.rem(r // 2, SIDE)
    xx = r // (2 * SIDE)
    other = 1 - core
    a = other * xx + core * yy
    b = core * xx + other * yy
    rows, total_cols = w_ref.shape
    kids = child_ref.shape[0]

    def mult8(v, m=8):
        return pl.multiple_of(v, m)

    def at(first, second):
        px = other * first + core * second
        py = core * first + other * second
        return (px * SIDE + py) * 2 + core

    load = pltpu.make_async_copy(front_ref, w_ref, local_sem.at[0])
    load.start()

    barrier = pltpu.get_barrier_semaphore()

    def greet(d, carry):
        pl.semaphore_signal(
            barrier, inc=1, device_id={"row": lax.rem(r + d, count)}, device_id_type=MESH
        )
        return carry

    lax.fori_loop(1, count, greet, 0)
    z_up, z_dn = lax.rem(z + 1, deep), lax.rem(z + deep - 1, deep)
    for peer in (z_up, z_dn):
        pl.semaphore_signal(barrier, inc=1, device_id={"col": peer}, device_id_type=MESH)

    orow = orow_ref[...]
    earlier = lax.broadcasted_iota(jnp.int32, (kids, kids), 0) < lax.broadcasted_iota(
        jnp.int32, (kids, kids), 1
    )
    same = jnp.logical_and(ocol_ref[...] == orow, earlier)
    rank = jnp.sum(jnp.where(same, 1.0, 0.0), axis=0, keepdims=True).astype(jnp.int32)
    slot = orow * 8 + rank * 2
    boxes = 8 * count
    box_id = lax.broadcasted_iota(jnp.int32, (boxes, kids), 0)
    even = jnp.where(box_id == slot, 1.0, 0.0)
    odd = jnp.where(box_id == slot + 1, 1.0, 0.0)
    filled = even + odd
    offset = jnp.sum(filled * off_ref[...], axis=1, keepdims=True)
    offset = offset + jnp.sum(filled, axis=1, keepdims=True) - 1.0
    outbox[:, pl.ds(0, TAG)] = jnp.broadcast_to(offset, (boxes, TAG))
    choose = jnp.concatenate([even, odd], axis=1).astype(BF16)

    def pack(m):
        lo = pl.multiple_of(m * 2 * HC, HC)
        both = jnp.concatenate(
            [child_ref[:, pl.ds(lo, HC)], child_ref[:, pl.ds(pl.multiple_of(lo + HC, HC), HC)]],
            axis=0,
        )
        outbox[:, pl.ds(pl.multiple_of(TAG + m * HC, TAG), HC)] = place(choose, both)

    nblk = total_cols // (2 * HC)
    bands = [
        (0, TAG + HC),
        (TAG + HC, 3 * HC),
        (TAG + 4 * HC, (nblk - 4) * HC),
    ]

    def mail(band, d):
        peer = lax.rem(r + d, count)
        cols = pl.ds(*bands[band])
        return pltpu.make_async_remote_copy(
            src_ref=outbox.at[pl.ds(mult8(8 * peer), 8), cols],
            dst_ref=inbox.at[pl.ds(mult8(8 * r), 8), cols],
            send_sem=box_send.at[band, d],
            recv_sem=box_recv.at[band, d],
            device_id={"row": peer},
            device_id_type=MESH,
        )

    def over_peers(action):
        def body(d, carry):
            action(d)
            return carry

        lax.fori_loop(1, count, body, 0)

    def post(band):
        over_peers(lambda d: mail(band, d).start())
        mine = pl.ds(mult8(8 * r), 8)
        cols = pl.ds(*bands[band])
        inbox[mine, cols] = outbox[mine, cols]

    def collect(band):
        over_peers(lambda d: mail(band, d).wait_recv())

    pack(0)
    pl.semaphore_wait(barrier, count - 1 + 2)
    post(0)
    for m in range(1, 4):
        pack(m)
    post(1)
    for m in range(4, nblk):
        pack(m)
    post(2)

    collect(0)
    place_at = jnp.transpose(inbox[:, pl.ds(0, TAG)])[0:1, :]
    row_id = lax.broadcasted_iota(jnp.int32, (rows, boxes), 0).astype(F32)
    parity = lax.rem(lax.broadcasted_iota(jnp.int32, (rows, boxes), 1), 2)
    hit = row_id == place_at
    for h in range(2):
        onehot[h] = jnp.where(jnp.logical_and(hit, parity == h), 1.0, 0.0).astype(BF16)

    def assemble(m):
        value = inbox[:, pl.ds(pl.multiple_of(TAG + m * HC, TAG), HC)]
        high, mid, low = split3(value)
        for h in range(2):
            hot = onehot[h]
            cols = pl.ds(pl.multiple_of((2 * m + h) * HC, HC), HC)
            added = jnp.dot(hot, high, preferred_element_type=F32) + (
                jnp.dot(hot, mid, preferred_element_type=F32)
                + jnp.dot(hot, low, preferred_element_type=F32)
            )
            w_ref[:, cols] = w_ref[:, cols] + added

    load.wait()
    assemble(0)

    nz = rows // 2 // ZROWS

    def pass_on(way, q):
        start = (q if way == 0 else nz + q) * ZROWS
        piece = a1_ref.at[pl.ds(start, ZROWS), :]
        return pltpu.make_async_remote_copy(
            src_ref=piece,
            dst_ref=piece,
            send_sem=z_send.at[way, q],
            recv_sem=z_recv.at[way, q],
            device_id={"col": z_up if way == 0 else z_dn},
            device_id_type=MESH,
        )

    @pl.when(z == 0)
    def _():
        a1_ref[...] = w_ref[:, pl.ds(0, WIDE)]
        for q in range(nz):
            for way in range(2):
                pass_on(way, q).start()

    for near in range(2):
        @pl.when(z == (1 if near == 0 else deep - 1))
        def _():
            for q in range(nz):
                pass_on(near, q).wait_recv()
                pass_on(near, q).start()
            for q in range(nz):
                pass_on(1 - near, q).wait_recv()

    @pl.when(z == 2)
    def _():
        for q in range(nz):
            for way in range(2):
                pass_on(way, q).wait_recv()
                pass_on(way, q).start()

    a1_save = pltpu.make_async_copy(a1_ref, a1_out, local_sem.at[1])
    a1_save.start()
    a1t = jnp.transpose(a1_ref[...])
    hi, lo = split(a1t)
    ah[...] = hi
    al[...] = lo
    p_ref[:, pl.ds(0, WIDE)] = product(a1t, a1_ref[...])

    a_up, a_dn, a_op = lax.rem(a + 1, SIDE), lax.rem(a + 3, SIDE), lax.rem(a + 2, SIDE)
    b_up, b_dn, b_op = lax.rem(b + 1, SIDE), lax.rem(b + 3, SIDE), lax.rem(b + 2, SIDE)
    dev = {
        "p": r + 1 - 2 * core,
        "a+": at(a_up, b),
        "a-": at(a_dn, b),
        "ao": at(a_op, b),
        "b+": at(a, b_up),
        "b-": at(a, b_dn),
        "bo": at(a, b_op),
    }
    chunks = [(0, WIDE)] + [(WIDE + i * CW, CW) for i in range(total_cols // CW)]
    n = len(chunks)
    started = {}
    saves = []

    def send(c, slot, src, dst, where):
        copy = pltpu.make_async_remote_copy(
            src_ref=src,
            dst_ref=dst,
            send_sem=send_sem.at[c, slot],
            recv_sem=recv_sem.at[c, slot],
            device_id={"row": dev[where]},
            device_id_type=MESH,
        )
        copy.start()
        started[(c, slot)] = copy

    def got(c, *slots):
        for slot in slots:
            started[(c, slot)].wait_recv()

    own = HALF * core

    def shard(i, half=0):
        return mult8(own + SHARD * i + half * (SHARD // 2))

    def sub(i, half=0):
        return mult8(own + SHARD * a + SUB * i + half * (SUB // 2))

    s32, s8 = SHARD // 2, SUB // 2

    def fill(c):
        if c == 2:
            collect(1)
            for m in range(1, 4):
                assemble(m)
        if c == 5:
            collect(2)
            for m in range(4, nblk):
                assemble(m)
            save = pltpu.make_async_copy(w_ref, w_out, local_sem.at[2])
            save.start()
            saves.append(save)
        for i in range(CW // 256):
            off = (c - 1) * CW + i * 256
            wh, wl = split(w_ref[:, pl.ds(off, 256)])
            p_ref[:, pl.ds(off + WIDE, 256)] = dot3(ah[...], al[...], wh, wl)

    def tools(c):
        cols = pl.ds(*chunks[c])

        def part(row, size):
            return p_ref.at[pl.ds(row, size), cols]

        def full(row, size):
            return f_ref.at[pl.ds(row, size), cols]

        def add(row, size, *sources, into=p_ref):
            span = pl.ds(row, size)
            value = p_ref[span, cols]
            for source in sources:
                value = value + source[...]
            into[span, cols] = value

        def one(i, size=s32):
            return r1.at[pl.ds(i * size, size), cols]

        def two(i, size=s8):
            return r2.at[pl.ds(i * size, size), cols]

        return cols, part, full, add, one, two

    def phase_gram(p):
        c = 0
        cols, part, full, add, one, two = tools(c)
        if p == 0:
            send(c, 0, part(mult8(HALF * other), HALF), r0.at[:, cols], "p")
        elif p == 1:
            got(c, 0)
            add(mult8(own), HALF, r0.at[:, cols])
            send(c, 1, part(shard(a_op), SHARD), one(0, SHARD), "ao")
            send(c, 2, part(shard(a_up), SHARD), one(1, SHARD), "a+")
            send(c, 3, part(shard(a_dn), SHARD), one(2, SHARD), "a-")
        elif p == 2:
            got(c, 2, 3, 1)
            add(shard(a), SHARD, one(0, SHARD), one(1, SHARD), one(2, SHARD))
            send(c, 4, part(sub(b_op), SUB), two(0, SUB), "bo")
            send(c, 5, part(sub(b_up), SUB), two(1, SUB), "b+")
            send(c, 6, part(sub(b_dn), SUB), two(2, SUB), "b-")
        elif p == 3:
            got(c, 5, 6, 4)
            add(sub(b), SUB, two(0, SUB), two(1, SUB), two(2, SUB), into=f_ref)
            for slot, where in ((7, "bo"), (8, "b+"), (9, "b-")):
                send(c, slot, full(sub(b), SUB), full(sub(b), SUB), where)
        elif p == 4:
            got(c, 8, 9, 7)
            for slot, where in ((10, "ao"), (11, "a+"), (12, "a-")):
                send(c, slot, full(shard(a), SHARD), full(shard(a), SHARD), where)
        elif p == 5:
            got(c, 11, 12, 10)
            send(c, 13, full(mult8(own), HALF), full(mult8(own), HALF), "p")
        elif p == 6:
            got(c, 13)

    def phase(c, p):
        cols, part, full, add, one, two = tools(c)
        if p == 0:
            fill(c)
            send(c, 0, part(mult8(HALF * other), HALF), r0.at[:, cols], "p")
        elif p == 1:
            got(c, 0)
            add(mult8(own), HALF, r0.at[:, cols])
            send(c, 1, part(shard(a_op, 0), s32), one(0), "a+")
            send(c, 2, part(shard(a_op, 1), s32), one(1), "a-")
            send(c, 3, part(shard(a_up, 1), s32), one(2), "a+")
            send(c, 4, part(shard(a_dn, 0), s32), one(3), "a-")
        elif p == 2:
            got(c, 1)
            add(shard(a_up, 0), s32, one(0))
            send(c, 5, part(shard(a_up, 0), s32), one(4), "a+")
            got(c, 2)
            add(shard(a_dn, 1), s32, one(1))
            send(c, 6, part(shard(a_dn, 1), s32), one(5), "a-")
        elif p == 3:
            got(c, 3, 4, 5, 6)
            add(shard(a, 0), s32, one(3), one(4))
            add(shard(a, 1), s32, one(2), one(5))
            send(c, 7, part(sub(b_op, 0), s8), two(0), "b+")
            send(c, 8, part(sub(b_op, 1), s8), two(1), "b-")
            send(c, 9, part(sub(b_up, 1), s8), two(2), "b+")
            send(c, 10, part(sub(b_dn, 0), s8), two(3), "b-")
        elif p == 4:
            got(c, 7)
            add(sub(b_up, 0), s8, two(0))
            send(c, 11, part(sub(b_up, 0), s8), two(4), "b+")
            got(c, 8)
            add(sub(b_dn, 1), s8, two(1))
            send(c, 12, part(sub(b_dn, 1), s8), two(5), "b-")
        elif p == 5:
            got(c, 9, 10, 11, 12)
            add(sub(b, 0), s8, two(3), two(4), into=f_ref)
            add(sub(b, 1), s8, two(2), two(5), into=f_ref)
            send(c, 13, full(sub(b), SUB), full(sub(b), SUB), "b+")
            send(c, 14, full(sub(b), SUB), full(sub(b), SUB), "b-")
        elif p == 6:
            got(c, 13)
            send(c, 15, full(sub(b_dn, 0), s8), full(sub(b_dn, 0), s8), "b+")
            got(c, 14)
            send(c, 16, full(sub(b_up, 1), s8), full(sub(b_up, 1), s8), "b-")
        elif p == 7:
            got(c, 15, 16)
            send(c, 17, full(shard(a), SHARD), full(shard(a), SHARD), "a+")
            send(c, 18, full(shard(a), SHARD), full(shard(a), SHARD), "a-")
        elif p == 8:
            got(c, 17)
            send(c, 19, full(shard(a_dn, 0), s32), full(shard(a_dn, 0), s32), "a+")
            got(c, 18)
            send(c, 20, full(shard(a_up, 1), s32), full(shard(a_up, 1), s32), "a-")
        elif p == 9:
            got(c, 19, 20)
            send(c, 21, full(mult8(own), HALF), full(mult8(own), HALF), "p")
        elif p == 10:
            got(c, 21)
            save = pltpu.make_async_copy(
                f_ref.at[:, cols],
                f_out.at[:, pl.ds((c - 1) * CW, CW)],
                local_sem.at[2 + c],
            )
            save.start()
            saves.append(save)

    def chol_begin(k):
        if k == 0:
            g_ref[...] = f_ref[:, pl.ds(0, WIDE)]
            linv_ref[...] = jnp.zeros_like(linv_ref)
        d = pl.ds(k * PB, PB)
        dblk[...] = g_ref[d, d]
        xblk[...] = jnp.where(
            lax.broadcasted_iota(jnp.int32, (PB, PB), 0)
            == lax.broadcasted_iota(jnp.int32, (PB, PB), 1),
            1.0,
            0.0,
        ).astype(F32)

    def chol_end(k):
        d = pl.ds(k * PB, PB)
        x = xblk[...]
        if k:
            left = pl.ds(0, k * PB)
            linv_ref[d, left] = -product(x, product(g_ref[d, left], linv_ref[left, left]))
        linv_ref[d, d] = x
        if k < PANELS - 1:
            rest = pl.ds((k + 1) * PB, (PANELS - 1 - k) * PB)
            below = tdot(g_ref[rest, d], x)
            g_ref[rest, d] = below
            g_ref[rest, rest] = g_ref[rest, rest] - tdot(below, below)

    pieces = []
    for k in range(PANELS):
        for q in range(PIECES):
            pieces.append((k, q))

    def piece(k, q):
        if q == 0:
            chol_begin(k)
        chol_steps(dblk, xblk, q * (PB // PIECES), (q + 1) * (PB // PIECES))
        if q == PIECES - 1:
            chol_end(k)

    steps = [(GRAM_TAU[p], 0, p) for p in range(7)]
    steps += [(2 * p + c, c, p) for c in range(1, n) for p in range(11)]
    before = None
    ready = False
    for tau, c, p in sorted(steps):
        if ready and tau != before and pieces:
            piece(*pieces.pop(0))
        before = tau
        if c == 0:
            phase_gram(p)
        else:
            phase(c, p)
        ready = ready or (c, p) == (0, 6)
    for rest in pieces:
        piece(*rest)

    for copy in started.values():
        copy.wait_send()
    for band in range(len(bands)):
        over_peers(lambda d: mail(band, d).wait_send())
    for way in range(2):
        end = deep - 1 if way == 0 else 1

        @pl.when(z != end)
        def _():
            for q in range(nz):
                pass_on(way, q).wait_send()

    a1_save.wait()
    for save in saves:
        save.wait()


def all_reduced(front, child, owner, offset):
    rows, cols = front.shape
    kids = child.shape[0]
    count, deep = lax.axis_size("row"), lax.axis_size("col")
    wide = cols + WIDE
    n = 1 + cols // CW
    vm = pl.BlockSpec(memory_space=pltpu.VMEM)
    hbm = pl.BlockSpec(memory_space=pl.ANY)
    dma = pltpu.SemaphoreType.DMA
    box = TAG + cols // 2
    return pl.pallas_call(
        main_kernel,
        out_shape=(
            jax.ShapeDtypeStruct((rows, cols), F32),
            jax.ShapeDtypeStruct((WIDE, cols), F32),
            jax.ShapeDtypeStruct((rows, WIDE), F32),
            jax.ShapeDtypeStruct((WIDE, WIDE), F32),
        ),
        in_specs=[vm, vm, vm, vm, hbm],
        out_specs=(hbm, hbm, hbm, vm),
        scratch_shapes=[
            pltpu.VMEM((rows, cols), F32),
            pltpu.VMEM((WIDE, wide), F32),
            pltpu.VMEM((WIDE, wide), F32),
            pltpu.VMEM((rows, WIDE), F32),
            pltpu.VMEM((WIDE, rows), BF16),
            pltpu.VMEM((WIDE, rows), BF16),
            pltpu.VMEM((HALF, wide), F32),
            pltpu.VMEM((6 * SHARD // 2, wide), F32),
            pltpu.VMEM((6 * SUB // 2, wide), F32),
            pltpu.VMEM((WIDE, WIDE), F32),
            pltpu.VMEM((PB, PB), F32),
            pltpu.VMEM((PB, PB), F32),
            pltpu.VMEM((8 * count, box), F32),
            pltpu.VMEM((8 * count, box), F32),
            pltpu.VMEM((2, rows, 8 * count), BF16),
            dma((n, COPIES)),
            dma((n, COPIES)),
            dma((3, count)),
            dma((3, count)),
            dma((2, rows // 2 // ZROWS)),
            dma((2, rows // 2 // ZROWS)),
            dma((2 + n,)),
        ],
        compiler_params=pltpu.CompilerParams(
            collective_id=0, has_side_effects=True, vmem_limit_bytes=63 * 1024 * 1024
        ),
        name="assemble_and_reduce",
    )(
        child,
        owner,
        owner.reshape(1, kids),
        offset.reshape(1, kids).astype(F32),
        front,
    )


def tail_kernel(scale, a1_ref, linv_ref, s_ref, w_ref, u_ref, o_ref, q_ref, lh, ll, qh, ql):
    @pl.when(pl.program_id(0) == 0)
    def _():
        linv = linv_ref[...]
        hi, lo = split(linv)
        lh[...] = hi
        ll[...] = lo
        basis = tdot(a1_ref[...], linv)
        q_ref[...] = basis * scale
        hi, lo = split(basis)
        qh[...] = hi
        ql[...] = lo

    sh, sl = split(s_ref[...])
    u = dot3(lh[...], ll[...], sh, sl)
    u_ref[...] = u
    uh, ul = split(u)
    o_ref[...] = w_ref[...] - dot3(qh[...], ql[...], uh, ul)


def tail(a1, linv, sums, w, scale):
    rows, cols = w.shape
    tc = 512
    whole = lambda shape: pl.BlockSpec(shape, lambda i: (0, 0))
    return pl.pallas_call(
        functools.partial(tail_kernel, scale),
        grid=(cols // tc,),
        out_shape=(
            jax.ShapeDtypeStruct((WIDE, cols), F32),
            jax.ShapeDtypeStruct((rows, cols), F32),
            jax.ShapeDtypeStruct((rows, WIDE), F32),
        ),
        in_specs=[
            whole((rows, WIDE)),
            whole((WIDE, WIDE)),
            pl.BlockSpec((WIDE, tc), lambda i: (0, i)),
            pl.BlockSpec((rows, tc), lambda i: (0, i)),
        ],
        out_specs=(
            pl.BlockSpec((WIDE, tc), lambda i: (0, i)),
            pl.BlockSpec((rows, tc), lambda i: (0, i)),
            whole((rows, WIDE)),
        ),
        scratch_shapes=[
            pltpu.VMEM((WIDE, WIDE), BF16),
            pltpu.VMEM((WIDE, WIDE), BF16),
            pltpu.VMEM((rows, WIDE), BF16),
            pltpu.VMEM((rows, WIDE), BF16),
        ],
        compiler_params=pltpu.CompilerParams(vmem_limit_bytes=40 * 1024 * 1024),
        name="project_out",
    )(a1, linv, sums, w)


def on_device(front_matrix, child_rows, child_owner, child_offset):
    total_rows = front_matrix.shape[0] * lax.axis_size("row")
    current, sums, panel, linv = all_reduced(front_matrix, child_rows, child_owner, child_offset)
    return tail(panel, linv, sums, current, math.sqrt(total_rows))


def solution(mesh):
    placed = (P("row", "col"), P("row", "col"), P("row", None), P("row", None))
    return jax.shard_map(
        on_device,
        mesh=mesh,
        in_specs=placed,
        out_specs=(P(None, "col"), P("row", "col"), P("row", None)),
        check_vma=False,
    )
```

time: 257 us -> 156 us (0.61)
  the two profiles are of different devices: /device:TPU:1 before, /device:TPU:33 now
where the time goes in v3:
time: 156 us
  Pallas kernels  148 us (95%)
  local copies, waits for them, and re-layouts  6.49 us (4%)
    pallas_call x1, Pallas kernels, all_reduced(): pl.pallas_call(main_kernel, out_shape=(jax.ShapeDtypeStruct((rows, cols),...  130 us
    pallas_call x1, Pallas kernels, tail(): pl.pallas_call(functools.partial(tail_kernel, scale), grid=(cols // tc,),...  17.6 us
    unnamed x7, local copies, waits for them, and re-layouts  6.49 us

profile of v3, /device:TPU:33, one launch (start us, length us, event | category | flops | bytes accessed | tf_op | source)
XLA Modules:
  0.0 156.0 jit_solution(10171843902414329733)
XLA Ops:
  0.6 1.2 convert_bitcast_fusion.off_ref
  1.8 1.4 copy.7.ocol_ref
  3.2 130.0 %assemble_and_reduce.1 = (f32[384,4096]{1,0:T(8,128)}, f32[512,4096]{1,0:T(8,128)}, f32[384,512]{1,0:T(8,128)}, f32[512,512]{1,0:T(8,128)}) custom-call(f32[64,4096]{1,0:T(8,128)} %child_ref.1, s32[64,1]{1,0:T(8,128)} %copy.7.ocol_ref, s32[1,64]{1,0:T(1,128)} %bitcast.3, f32[1,64]{1,0:T(1,128)} %convert_bitcast_fusion.off_ref, f32[384,4096]{1,0:T(8,128)} %front_ref.1), custom_call_target="tpu_custom_call" | custom-call | tf_op jit(solution)/shard_map/assemble_and_reduce/pallas_call | solution.py:563
  133.2 0.0 copy-start
  133.2 2.8 %copy-done = f32[384,4096]{1,0:T(8,128)S(1)} copy-done((f32[384,4096]{1,0:T(8,128)S(1)}, f32[384,4096]{1,0:T(8,128)}, u32[]{:S(2)}) %copy-start) | copy-done | bytes 6291480
  136.0 0.0 copy-start.1
  136.0 1.2 copy-done.1
  137.2 0.0 copy-start.2
  137.2 1.1 copy-done.2
  138.3 17.6 %project_out.1 = (f32[512,4096]{1,0:T(8,128)}, f32[384,4096]{1,0:T(8,128)}, f32[384,512]{1,0:T(8,128)}) custom-call(f32[384,512]{1,0:T(8,128)S(1)} %copy-done.2, f32[512,512]{1,0:T(8,128)S(1)} %copy-done.1, f32[512,4096]{1,0:T(8,128)} %get-tuple-element.9.s_ref, f32[384,4096]{1,0:T(8,128)S(1)} %copy-done), custom_call_target="tpu_custom_call" | custom-call | tf_op jit(solution)/shard_map/project_out/pallas_call | solution.py:634
Async XLA Ops:
  133.2 2.8 %copy-start = (f32[384,4096]{1,0:T(8,128)S(1)}, f32[384,4096]{1,0:T(8,128)}, u32[]{:S(2)}) copy-start(f32[384,4096]{1,0:T(8,128)} %get-tuple-element.10.w_ref) | copy-start | bytes 18874372
  136.0 1.2 copy-start.1
  137.2 1.1 copy-start.2

commit v4 on v3

--- a/solution.py
+++ b/solution.py
@@ -26,6 +26,7 @@
 PIECES = 4
 COPIES = 22
 ZROWS = 32
+BROWS = 64
 
 
 def product(left_op, right_op):
@@ -118,8 +119,8 @@
 def main_kernel(
     child_ref, ocol_ref, orow_ref, off_ref, front_ref,
     w_out, f_out, a1_out, linv_ref,
-    w_ref, f_ref, p_ref, a1_ref, ah, al, r0, r1, r2, g_ref, dblk, xblk,
-    outbox, inbox, onehot,
+    w_ref, f_ref, p_ref, a1_ref, a1_full, ah, al, r0, r1, r2, g_ref, dblk, xblk,
+    outbox, inbox, zbox, onehot, lh, ll, u_ref,
     send_sem, recv_sem, box_send, box_recv, z_send, z_recv, local_sem,
 ):
     count = lax.axis_size("row")
@@ -142,6 +143,12 @@
         px = other * first + core * second
         py = core * first + other * second
         return (px * SIDE + py) * 2 + core
+
+    first = pltpu.make_async_copy(front_ref.at[:, pl.ds(0, WIDE)], a1_ref, local_sem.at[1])
+
+    @pl.when(z == 0)
+    def _():
+        first.start()
 
     load = pltpu.make_async_copy(front_ref, w_ref, local_sem.at[0])
     load.start()
@@ -191,45 +198,112 @@
         (TAG + 4 * HC, (nblk - 4) * HC),
     ]
 
-    def mail(band, d):
-        peer = lax.rem(r + d, count)
+    peers = [
+        (dx, dy, dc)
+        for dc in (1, 0)
+        for dy in range(SIDE)
+        for dx in (1, 3, 2, 0)
+        if (dx, dy, dc) != (0, 0, 0)
+    ]
+    turn = 1 - 2 * core
+
+    def mail(band, k):
+        dx, dy, dc = peers[k]
+        px = lax.rem(xx + turn * dx + SIDE, SIDE)
+        py = lax.rem(yy + turn * dy + SIDE, SIDE)
+        peer = (px * SIDE + py) * 2 + lax.rem(core + dc, 2)
         cols = pl.ds(*bands[band])
         return pltpu.make_async_remote_copy(
             src_ref=outbox.at[pl.ds(mult8(8 * peer), 8), cols],
             dst_ref=inbox.at[pl.ds(mult8(8 * r), 8), cols],
-            send_sem=box_send.at[band, d],
-            recv_sem=box_recv.at[band, d],
+            send_sem=box_send.at[band, k],
+            recv_sem=box_recv.at[band, k],
             device_id={"row": peer},
             device_id_type=MESH,
         )
 
     def over_peers(action):
-        def body(d, carry):
-            action(d)
-            return carry
-
-        lax.fori_loop(1, count, body, 0)
+        for k in range(len(peers)):
+            action(k)
 
     def post(band):
-        over_peers(lambda d: mail(band, d).start())
+        over_peers(lambda k: mail(band, k).start())
         mine = pl.ds(mult8(8 * r), 8)
         cols = pl.ds(*bands[band])
         inbox[mine, cols] = outbox[mine, cols]
 
     def collect(band):
-        over_peers(lambda d: mail(band, d).wait_recv())
+        over_peers(lambda k: mail(band, k).wait_recv())
+
+    na, nb = rows // 2 // ZROWS, boxes // 2 // BROWS
+
+    def pass_on(way, q):
+        if q < na:
+            piece = a1_ref.at[pl.ds((way * na + q) * ZROWS, ZROWS), :]
+        else:
+            piece = zbox.at[pl.ds((way * nb + q - na) * BROWS, BROWS), :]
+        return pltpu.make_async_remote_copy(
+            src_ref=piece,
+            dst_ref=piece,
+            send_sem=z_send.at[way, q],
+            recv_sem=z_recv.at[way, q],
+            device_id={"col": z_up if way == 0 else z_dn},
+            device_id_type=MESH,
+        )
+
+    def source(span):
+        @pl.when(z == 0)
+        def _():
+            for q in span:
+                for way in range(2):
+                    pass_on(way, q).start()
+
+    def near(span):
+        for way in range(2):
+            @pl.when(z == (1 if way == 0 else deep - 1))
+            def _():
+                for q in span:
+                    pass_on(way, q).wait_recv()
+                    pass_on(way, q).start()
+
+        @pl.when(z == 2)
+        def _():
+            for q in span:
+                for way in range(2):
+                    pass_on(way, q).wait_recv()
+                    pass_on(way, q).start()
+
+    def far(span):
+        for way in range(2):
+            @pl.when(z == (1 if way == 1 else deep - 1))
+            def _():
+                for q in span:
+                    pass_on(way, q).wait_recv()
 
     pack(0)
+
+    @pl.when(z == 0)
+    def _():
+        first.wait()
+
     pl.semaphore_wait(barrier, count - 1 + 2)
     post(0)
+    source(range(na))
     for m in range(1, 4):
         pack(m)
     post(1)
     for m in range(4, nblk):
         pack(m)
     post(2)
+    near(range(na))
 
     collect(0)
+
+    @pl.when(z == 0)
+    def _():
+        zbox[...] = inbox[:, pl.ds(TAG, HC)]
+
+    source(range(na, na + nb))
     place_at = jnp.transpose(inbox[:, pl.ds(0, TAG)])[0:1, :]
     row_id = lax.broadcasted_iota(jnp.int32, (rows, boxes), 0).astype(F32)
     parity = lax.rem(lax.broadcasted_iota(jnp.int32, (rows, boxes), 1), 2)
@@ -249,53 +323,22 @@
             )
             w_ref[:, cols] = w_ref[:, cols] + added
 
+    near(range(na, na + nb))
     load.wait()
     assemble(0)
-
-    nz = rows // 2 // ZROWS
-
-    def pass_on(way, q):
-        start = (q if way == 0 else nz + q) * ZROWS
-        piece = a1_ref.at[pl.ds(start, ZROWS), :]
-        return pltpu.make_async_remote_copy(
-            src_ref=piece,
-            dst_ref=piece,
-            send_sem=z_send.at[way, q],
-            recv_sem=z_recv.at[way, q],
-            device_id={"col": z_up if way == 0 else z_dn},
-            device_id_type=MESH,
-        )
-
-    @pl.when(z == 0)
-    def _():
-        a1_ref[...] = w_ref[:, pl.ds(0, WIDE)]
-        for q in range(nz):
-            for way in range(2):
-                pass_on(way, q).start()
-
-    for near in range(2):
-        @pl.when(z == (1 if near == 0 else deep - 1))
-        def _():
-            for q in range(nz):
-                pass_on(near, q).wait_recv()
-                pass_on(near, q).start()
-            for q in range(nz):
-                pass_on(1 - near, q).wait_recv()
-
-    @pl.when(z == 2)
-    def _():
-        for q in range(nz):
-            for way in range(2):
-                pass_on(way, q).wait_recv()
-                pass_on(way, q).start()
-
-    a1_save = pltpu.make_async_copy(a1_ref, a1_out, local_sem.at[1])
+    far(range(na + nb))
+    value = zbox[...]
+    for h in range(2):
+        cols = pl.ds(h * HC, HC)
+        a1_full[:, cols] = a1_ref[:, cols] + place(onehot[h], value)
+
+    a1_save = pltpu.make_async_copy(a1_full, a1_out, local_sem.at[1])
     a1_save.start()
-    a1t = jnp.transpose(a1_ref[...])
+    a1t = jnp.transpose(a1_full[...])
     hi, lo = split(a1t)
     ah[...] = hi
     al[...] = lo
-    p_ref[:, pl.ds(0, WIDE)] = product(a1t, a1_ref[...])
+    p_ref[:, pl.ds(0, WIDE)] = product(a1t, a1_full[...])
 
     a_up, a_dn, a_op = lax.rem(a + 1, SIDE), lax.rem(a + 3, SIDE), lax.rem(a + 2, SIDE)
     b_up, b_dn, b_op = lax.rem(b + 1, SIDE), lax.rem(b + 3, SIDE), lax.rem(b + 2, SIDE)
@@ -471,13 +514,7 @@
             send(c, 21, full(mult8(own), HALF), full(mult8(own), HALF), "p")
         elif p == 10:
             got(c, 21)
-            save = pltpu.make_async_copy(
-                f_ref.at[:, cols],
-                f_out.at[:, pl.ds((c - 1) * CW, CW)],
-                local_sem.at[2 + c],
-            )
-            save.start()
-            saves.append(save)
+            summed.append(c)
 
     def chol_begin(k):
         if k == 0:
@@ -517,6 +554,30 @@
         if q == PIECES - 1:
             chol_end(k)
 
+    summed = []
+    emits = []
+
+    def emit(c):
+        slot = len(emits) % 2
+        if len(emits) > 1:
+            emits[-2].wait()
+        cols = pl.ds(*chunks[c])
+        top = pl.ds(0, HALF)
+        low = pl.ds(HALF, HALF)
+        fh, fl = split(f_ref[:, cols])
+        u_ref[slot, top] = dot3(lh[top, top], ll[top, top], fh[:HALF], fl[:HALF])
+        u_ref[slot, low] = dot3(lh[low, :], ll[low, :], fh, fl)
+        out = pltpu.make_async_copy(
+            u_ref.at[slot], f_out.at[:, pl.ds((c - 1) * CW, CW)], local_sem.at[2 + c]
+        )
+        out.start()
+        emits.append(out)
+
+    def ready_factor():
+        hi, lo = split(linv_ref[...])
+        lh[...] = hi
+        ll[...] = lo
+
     steps = [(GRAM_TAU[p], 0, p) for p in range(7)]
     steps += [(2 * p + c, c, p) for c in range(1, n) for p in range(11)]
     before = None
@@ -524,6 +585,12 @@
     for tau, c, p in sorted(steps):
         if ready and tau != before and pieces:
             piece(*pieces.pop(0))
+            if not pieces:
+                ready_factor()
+        elif ready and tau != before:
+            for done in summed:
+                emit(done)
+            summed.clear()
         before = tau
         if c == 0:
             phase_gram(p)
@@ -532,17 +599,23 @@
         ready = ready or (c, p) == (0, 6)
     for rest in pieces:
         piece(*rest)
+    if pieces:
+        ready_factor()
+    for done in summed:
+        emit(done)
+    for out in emits[-2:]:
+        out.wait()
 
     for copy in started.values():
         copy.wait_send()
     for band in range(len(bands)):
-        over_peers(lambda d: mail(band, d).wait_send())
+        over_peers(lambda k: mail(band, k).wait_send())
     for way in range(2):
         end = deep - 1 if way == 0 else 1
 
         @pl.when(z != end)
         def _():
-            for q in range(nz):
+            for q in range(na + nb):
                 pass_on(way, q).wait_send()
 
     a1_save.wait()
@@ -560,6 +633,7 @@
     hbm = pl.BlockSpec(memory_space=pl.ANY)
     dma = pltpu.SemaphoreType.DMA
     box = TAG + cols // 2
+    rings = rows // 2 // ZROWS + 4 * count // BROWS
     return pl.pallas_call(
         main_kernel,
         out_shape=(
@@ -575,6 +649,7 @@
             pltpu.VMEM((WIDE, wide), F32),
             pltpu.VMEM((WIDE, wide), F32),
             pltpu.VMEM((rows, WIDE), F32),
+            pltpu.VMEM((rows, WIDE), F32),
             pltpu.VMEM((WIDE, rows), BF16),
             pltpu.VMEM((WIDE, rows), BF16),
             pltpu.VMEM((HALF, wide), F32),
@@ -585,13 +660,17 @@
             pltpu.VMEM((PB, PB), F32),
             pltpu.VMEM((8 * count, box), F32),
             pltpu.VMEM((8 * count, box), F32),
+            pltpu.VMEM((8 * count, HC), F32),
             pltpu.VMEM((2, rows, 8 * count), BF16),
+            pltpu.VMEM((WIDE, WIDE), BF16),
+            pltpu.VMEM((WIDE, WIDE), BF16),
+            pltpu.VMEM((2, WIDE, CW), F32),
             dma((n, COPIES)),
             dma((n, COPIES)),
             dma((3, count)),
             dma((3, count)),
-            dma((2, rows // 2 // ZROWS)),
-            dma((2, rows // 2 // ZROWS)),
+            dma((2, rings)),
+            dma((2, rings)),
             dma((2 + n,)),
         ],
         compiler_params=pltpu.CompilerParams(
@@ -607,30 +686,26 @@
     )
 
 
-def tail_kernel(scale, a1_ref, linv_ref, s_ref, w_ref, u_ref, o_ref, q_ref, lh, ll, qh, ql):
+def tail_kernel(scale, a1_ref, linv_ref, s_ref, w_ref, u_ref, o_ref, q_ref, qh, ql):
     @pl.when(pl.program_id(0) == 0)
     def _():
-        linv = linv_ref[...]
-        hi, lo = split(linv)
-        lh[...] = hi
-        ll[...] = lo
-        basis = tdot(a1_ref[...], linv)
+        basis = tdot(a1_ref[...], linv_ref[...])
         q_ref[...] = basis * scale
         hi, lo = split(basis)
         qh[...] = hi
         ql[...] = lo
 
-    sh, sl = split(s_ref[...])
-    u = dot3(lh[...], ll[...], sh, sl)
+    u = s_ref[...]
     u_ref[...] = u
     uh, ul = split(u)
     o_ref[...] = w_ref[...] - dot3(qh[...], ql[...], uh, ul)
 
 
-def tail(a1, linv, sums, w, scale):
+def tail(a1, linv, upper, w, scale):
     rows, cols = w.shape
     tc = 512
     whole = lambda shape: pl.BlockSpec(shape, lambda i: (0, 0))
+    tile = lambda size: pl.BlockSpec((size, tc), lambda i: (0, i))
     return pl.pallas_call(
         functools.partial(tail_kernel, scale),
         grid=(cols // tc,),
@@ -639,32 +714,18 @@
             jax.ShapeDtypeStruct((rows, cols), F32),
             jax.ShapeDtypeStruct((rows, WIDE), F32),
         ),
-        in_specs=[
-            whole((rows, WIDE)),
-            whole((WIDE, WIDE)),
-            pl.BlockSpec((WIDE, tc), lambda i: (0, i)),
-            pl.BlockSpec((rows, tc), lambda i: (0, i)),
-        ],
-        out_specs=(
-            pl.BlockSpec((WIDE, tc), lambda i: (0, i)),
-            pl.BlockSpec((rows, tc), lambda i: (0, i)),
-            whole((rows, WIDE)),
-        ),
-        scratch_shapes=[
-            pltpu.VMEM((WIDE, WIDE), BF16),
-            pltpu.VMEM((WIDE, WIDE), BF16),
-            pltpu.VMEM((rows, WIDE), BF16),
-            pltpu.VMEM((rows, WIDE), BF16),
-        ],
-        compiler_params=pltpu.CompilerParams(vmem_limit_bytes=40 * 1024 * 1024),
+        in_specs=[whole((rows, WIDE)), whole((WIDE, WIDE)), tile(WIDE), tile(rows)],
+        out_specs=(tile(WIDE), tile(rows), whole((rows, WIDE))),
+        scratch_shapes=[pltpu.VMEM((rows, WIDE), BF16), pltpu.VMEM((rows, WIDE), BF16)],
+        compiler_params=pltpu.CompilerParams(vmem_limit_bytes=62 * 1024 * 1024),
         name="project_out",
-    )(a1, linv, sums, w)
+    )(a1, linv, upper, w)
 
 
 def on_device(front_matrix, child_rows, child_owner, child_offset):
     total_rows = front_matrix.shape[0] * lax.axis_size("row")
-    current, sums, panel, linv = all_reduced(front_matrix, child_rows, child_owner, child_offset)
-    return tail(panel, linv, sums, current, math.sqrt(total_rows))
+    current, upper, panel, linv = all_reduced(front_matrix, child_rows, child_owner, child_offset)
+    return tail(panel, linv, upper, current, math.sqrt(total_rows))
 
 
 def solution(mesh):

time: 156 us -> 134 us (0.86)
  the two profiles are of different devices: /device:TPU:33 before, /device:TPU:1 now
where the time goes in v4:
time: 134 us; the launch traced here: 133 us
  Pallas kernels  130 us (97%)
  local copies, waits for them, and re-layouts  1.36 us (1%)
    pallas_call x1, Pallas kernels, all_reduced(): pl.pallas_call(main_kernel, out_shape=(jax.ShapeDtypeStruct((rows, cols),...  115 us
    pallas_call x1, Pallas kernels, tail(): pl.pallas_call(functools.partial(tail_kernel, scale), grid=(cols // tc,),...  15.7 us

profile of v4, /device:TPU:1, one launch (start us, length us, event | category | flops | bytes accessed | tf_op | source)
XLA Modules:
  0.0 133.4 jit_solution(8407195672582444729)
XLA Ops:
  0.6 1.2 convert_bitcast_fusion.off_ref
  1.8 1.4 %copy.7.ocol_ref = s32[64,1]{1,0:T(8,128)} copy(s32[64,1]{0,1:T(1,128)} %param.6) | data formatting | bytes 512 | tf_op args[2]
  3.2 114.5 %assemble_and_reduce.1 = (f32[384,4096]{1,0:T(8,128)}, f32[512,4096]{1,0:T(8,128)}, f32[384,512]{1,0:T(8,128)}, f32[512,512]{1,0:T(8,128)}) custom-call(f32[64,4096]{1,0:T(8,128)} %child_ref.1, s32[64,1]{1,0:T(8,128)} %copy.7.ocol_ref, s32[1,64]{1,0:T(1,128)} %bitcast.3, f32[1,64]{1,0:T(1,128)} %convert_bitcast_fusion.off_ref, f32[384,4096]{1,0:T(8,128)} %front_ref.1), custom_call_target="tpu_custom_call" | custom-call | tf_op jit(solution)/shard_map/assemble_and_reduce/pallas_call | solution.py:637
  117.7 15.7 %project_out.1 = (f32[512,4096]{1,0:T(8,128)}, f32[384,4096]{1,0:T(8,128)}, f32[384,512]{1,0:T(8,128)}) custom-call(f32[384,512]{1,0:T(8,128)} %get-tuple-element.7.a1_ref, f32[512,512]{1,0:T(8,128)} %get-tuple-element.8.linv_ref, f32[512,4096]{1,0:T(8,128)} %get-tuple-element.9.s_ref, f32[384,4096]{1,0:T(8,128)} %get-tuple-element.10.w_ref), custom_call_target="tpu_custom_call" | custom-call | tf_op jit(solution)/shard_map/project_out/pallas_call | solution.py:709

commit v5 on v4

--- a/solution.py
+++ b/solution.py
@@ -22,8 +22,8 @@
 HC = 256
 TAG = 128
 GROUP = 4
-GRAM_TAU = (-2, -1, 2, 3, 4, 5, 6)
 PIECES = 4
+GRAM_TAU = (-2, 0, 2, 4, 5.5, 7.5, 8.5)
 COPIES = 22
 ZROWS = 32
 BROWS = 64
@@ -64,13 +64,14 @@
 
 
 def chol_steps(dblk, xblk, start, stop):
-    lane = lax.broadcasted_iota(jnp.int32, (PB, PB), 1)
+    live = pl.ds(start, PB - start)
+    lane = lax.broadcasted_iota(jnp.int32, (PB - start, PB), 1)
     lane1 = lax.broadcasted_iota(jnp.int32, (1, PB), 1)
-    sub = lax.broadcasted_iota(jnp.int32, (PB, PB), 0)
+    sub = lax.broadcasted_iota(jnp.int32, (PB - start, PB), 0) + start
 
     def step(i, carry):
         j = i * GROUP
-        a, x = dblk[...], xblk[...]
+        a, x = dblk[live, :], xblk[live, :]
         span = range(GROUP)
         rows = [dblk[pl.ds(j + q, 1), :] for q in span]
         xrows = [xblk[pl.ds(j + q, 1), :] for q in span]
@@ -103,8 +104,8 @@
         nx = jnp.where(below, nx, x)
         for p in span:
             nx = jnp.where(sub == j + p, xrows[p] * invs[p], nx)
-        dblk[...] = jnp.where(below, na, a)
-        xblk[...] = nx
+        dblk[live, :] = jnp.where(below, na, a)
+        xblk[live, :] = nx
         return carry
 
     lax.fori_loop(start // GROUP, stop // GROUP, step, 0)
@@ -118,9 +119,9 @@
 
 def main_kernel(
     child_ref, ocol_ref, orow_ref, off_ref, front_ref,
-    w_out, f_out, a1_out, linv_ref,
+    w_out, f_out, q_ref, linv_ref,
     w_ref, f_ref, p_ref, a1_ref, a1_full, ah, al, r0, r1, r2, g_ref, dblk, xblk,
-    outbox, inbox, zbox, onehot, lh, ll, u_ref,
+    outbox, inbox, zbox, onehot,
     send_sem, recv_sem, box_send, box_recv, z_send, z_recv, local_sem,
 ):
     count = lax.axis_size("row")
@@ -332,8 +333,6 @@
         cols = pl.ds(h * HC, HC)
         a1_full[:, cols] = a1_ref[:, cols] + place(onehot[h], value)
 
-    a1_save = pltpu.make_async_copy(a1_full, a1_out, local_sem.at[1])
-    a1_save.start()
     a1t = jnp.transpose(a1_full[...])
     hi, lo = split(a1t)
     ah[...] = hi
@@ -385,12 +384,11 @@
     def fill(c):
         if c == 2:
             collect(1)
-            for m in range(1, 4):
-                assemble(m)
         if c == 5:
             collect(2)
-            for m in range(4, nblk):
-                assemble(m)
+        if c > 1:
+            assemble(c - 1)
+        if c == n - 1:
             save = pltpu.make_async_copy(w_ref, w_out, local_sem.at[2])
             save.start()
             saves.append(save)
@@ -478,30 +476,16 @@
             got(c, 3, 4, 5, 6)
             add(shard(a, 0), s32, one(3), one(4))
             add(shard(a, 1), s32, one(2), one(5))
-            send(c, 7, part(sub(b_op, 0), s8), two(0), "b+")
-            send(c, 8, part(sub(b_op, 1), s8), two(1), "b-")
-            send(c, 9, part(sub(b_up, 1), s8), two(2), "b+")
-            send(c, 10, part(sub(b_dn, 0), s8), two(3), "b-")
-        elif p == 4:
-            got(c, 7)
-            add(sub(b_up, 0), s8, two(0))
-            send(c, 11, part(sub(b_up, 0), s8), two(4), "b+")
-            got(c, 8)
-            add(sub(b_dn, 1), s8, two(1))
-            send(c, 12, part(sub(b_dn, 1), s8), two(5), "b-")
+            send(c, 7, part(sub(b_op), SUB), two(0, SUB), "bo")
+            send(c, 8, part(sub(b_up), SUB), two(1, SUB), "b+")
+            send(c, 9, part(sub(b_dn), SUB), two(2, SUB), "b-")
         elif p == 5:
-            got(c, 9, 10, 11, 12)
-            add(sub(b, 0), s8, two(3), two(4), into=f_ref)
-            add(sub(b, 1), s8, two(2), two(5), into=f_ref)
-            send(c, 13, full(sub(b), SUB), full(sub(b), SUB), "b+")
-            send(c, 14, full(sub(b), SUB), full(sub(b), SUB), "b-")
-        elif p == 6:
-            got(c, 13)
-            send(c, 15, full(sub(b_dn, 0), s8), full(sub(b_dn, 0), s8), "b+")
-            got(c, 14)
-            send(c, 16, full(sub(b_up, 1), s8), full(sub(b_up, 1), s8), "b-")
+            got(c, 8, 9, 7)
+            add(sub(b), SUB, two(0, SUB), two(1, SUB), two(2, SUB), into=f_ref)
+            for slot, where in ((13, "bo"), (14, "b+"), (15, "b-")):
+                send(c, slot, full(sub(b), SUB), full(sub(b), SUB), where)
         elif p == 7:
-            got(c, 15, 16)
+            got(c, 14, 15, 13)
             send(c, 17, full(shard(a), SHARD), full(shard(a), SHARD), "a+")
             send(c, 18, full(shard(a), SHARD), full(shard(a), SHARD), "a-")
         elif p == 8:
@@ -514,7 +498,11 @@
             send(c, 21, full(mult8(own), HALF), full(mult8(own), HALF), "p")
         elif p == 10:
             got(c, 21)
-            summed.append(c)
+            save = pltpu.make_async_copy(
+                f_ref.at[:, cols], f_out.at[:, pl.ds((c - 1) * CW, CW)], local_sem.at[2 + c]
+            )
+            save.start()
+            saves.append(save)
 
     def chol_begin(k):
         if k == 0:
@@ -554,32 +542,11 @@
         if q == PIECES - 1:
             chol_end(k)
 
-    summed = []
-    emits = []
-
-    def emit(c):
-        slot = len(emits) % 2
-        if len(emits) > 1:
-            emits[-2].wait()
-        cols = pl.ds(*chunks[c])
-        top = pl.ds(0, HALF)
-        low = pl.ds(HALF, HALF)
-        fh, fl = split(f_ref[:, cols])
-        u_ref[slot, top] = dot3(lh[top, top], ll[top, top], fh[:HALF], fl[:HALF])
-        u_ref[slot, low] = dot3(lh[low, :], ll[low, :], fh, fl)
-        out = pltpu.make_async_copy(
-            u_ref.at[slot], f_out.at[:, pl.ds((c - 1) * CW, CW)], local_sem.at[2 + c]
-        )
-        out.start()
-        emits.append(out)
-
     def ready_factor():
-        hi, lo = split(linv_ref[...])
-        lh[...] = hi
-        ll[...] = lo
+        q_ref[...] = tdot(a1_full[...], linv_ref[...])
 
     steps = [(GRAM_TAU[p], 0, p) for p in range(7)]
-    steps += [(2 * p + c, c, p) for c in range(1, n) for p in range(11)]
+    steps += [(2 * p + c - 1, c, p) for c in range(1, n) for p in (0, 1, 2, 3, 5, 7, 8, 9, 10)]
     before = None
     ready = False
     for tau, c, p in sorted(steps):
@@ -587,10 +554,6 @@
             piece(*pieces.pop(0))
             if not pieces:
                 ready_factor()
-        elif ready and tau != before:
-            for done in summed:
-                emit(done)
-            summed.clear()
         before = tau
         if c == 0:
             phase_gram(p)
@@ -601,10 +564,6 @@
         piece(*rest)
     if pieces:
         ready_factor()
-    for done in summed:
-        emit(done)
-    for out in emits[-2:]:
-        out.wait()
 
     for copy in started.values():
         copy.wait_send()
@@ -618,7 +577,6 @@
             for q in range(na + nb):
                 pass_on(way, q).wait_send()
 
-    a1_save.wait()
     for save in saves:
         save.wait()
 
@@ -643,7 +601,7 @@
             jax.ShapeDtypeStruct((WIDE, WIDE), F32),
         ),
         in_specs=[vm, vm, vm, vm, hbm],
-        out_specs=(hbm, hbm, hbm, vm),
+        out_specs=(hbm, hbm, vm, vm),
         scratch_shapes=[
             pltpu.VMEM((rows, cols), F32),
             pltpu.VMEM((WIDE, wide), F32),
@@ -662,9 +620,6 @@
             pltpu.VMEM((8 * count, box), F32),
             pltpu.VMEM((8 * count, HC), F32),
             pltpu.VMEM((2, rows, 8 * count), BF16),
-            pltpu.VMEM((WIDE, WIDE), BF16),
-            pltpu.VMEM((WIDE, WIDE), BF16),
-            pltpu.VMEM((2, WIDE, CW), F32),
             dma((n, COPIES)),
             dma((n, COPIES)),
             dma((3, count)),
@@ -686,25 +641,26 @@
     )
 
 
-def tail_kernel(scale, a1_ref, linv_ref, s_ref, w_ref, u_ref, o_ref, q_ref, qh, ql):
+def tail_kernel(scale, basis_ref, linv_ref, s_ref, w_ref, u_ref, o_ref, q_ref, qh, ql, lh, ll):
     @pl.when(pl.program_id(0) == 0)
     def _():
-        basis = tdot(a1_ref[...], linv_ref[...])
+        basis = basis_ref[...]
         q_ref[...] = basis * scale
-        hi, lo = split(basis)
-        qh[...] = hi
-        ql[...] = lo
-
-    u = s_ref[...]
-    u_ref[...] = u
-    uh, ul = split(u)
+        qh[...], ql[...] = split(basis)
+        lh[...], ll[...] = split(linv_ref[...])
+
+    fh, fl = split(s_ref[...])
+    top, low = pl.ds(0, HALF), pl.ds(HALF, HALF)
+    u_ref[top, :] = dot3(lh[top, top], ll[top, top], fh[:HALF], fl[:HALF])
+    u_ref[low, :] = dot3(lh[low, :], ll[low, :], fh, fl)
+    uh, ul = split(u_ref[...])
     o_ref[...] = w_ref[...] - dot3(qh[...], ql[...], uh, ul)
 
 
-def tail(a1, linv, upper, w, scale):
+def tail(basis, linv, sums, w, scale):
     rows, cols = w.shape
     tc = 512
-    whole = lambda shape: pl.BlockSpec(shape, lambda i: (0, 0))
+    whole = lambda size: pl.BlockSpec((size, WIDE), lambda i: (0, 0))
     tile = lambda size: pl.BlockSpec((size, tc), lambda i: (0, i))
     return pl.pallas_call(
         functools.partial(tail_kernel, scale),
@@ -714,18 +670,23 @@
             jax.ShapeDtypeStruct((rows, cols), F32),
             jax.ShapeDtypeStruct((rows, WIDE), F32),
         ),
-        in_specs=[whole((rows, WIDE)), whole((WIDE, WIDE)), tile(WIDE), tile(rows)],
-        out_specs=(tile(WIDE), tile(rows), whole((rows, WIDE))),
-        scratch_shapes=[pltpu.VMEM((rows, WIDE), BF16), pltpu.VMEM((rows, WIDE), BF16)],
+        in_specs=[whole(rows), whole(WIDE), tile(WIDE), tile(rows)],
+        out_specs=(tile(WIDE), tile(rows), whole(rows)),
+        scratch_shapes=[
+            pltpu.VMEM((rows, WIDE), BF16),
+            pltpu.VMEM((rows, WIDE), BF16),
+            pltpu.VMEM((WIDE, WIDE), BF16),
+            pltpu.VMEM((WIDE, WIDE), BF16),
+        ],
         compiler_params=pltpu.CompilerParams(vmem_limit_bytes=62 * 1024 * 1024),
         name="project_out",
-    )(a1, linv, upper, w)
+    )(basis, linv, sums, w)
 
 
 def on_device(front_matrix, child_rows, child_owner, child_offset):
     total_rows = front_matrix.shape[0] * lax.axis_size("row")
-    current, upper, panel, linv = all_reduced(front_matrix, child_rows, child_owner, child_offset)
-    return tail(panel, linv, upper, current, math.sqrt(total_rows))
+    current, sums, basis, linv = all_reduced(front_matrix, child_rows, child_owner, child_offset)
+    return tail(basis, linv, sums, current, math.sqrt(total_rows))
 
 
 def solution(mesh):

time: 134 us -> 127 us (0.948)
  Pallas kernels: 130 us -> 123 us
    pallas_call x1, Pallas kernels: 115 us -> 107 us  [all_reduced(): pl.pallas_call(main_kernel, out_shape=(jax.ShapeDtypeStruct((rows, cols),...]
where the time goes in v5:
time: 127 us
  Pallas kernels  123 us (97%)
  local copies, waits for them, and re-layouts  1.36 us (1%)
    pallas_call x1, Pallas kernels, all_reduced(): pl.pallas_call(main_kernel, out_shape=(jax.ShapeDtypeStruct((rows, cols),...  107 us
    pallas_call x1, Pallas kernels, tail(): pl.pallas_call(functools.partial(tail_kernel, scale), grid=(cols // tc,),...  16 us

profile of v5, /device:TPU:1, one launch (start us, length us, event | category | flops | bytes accessed | tf_op | source)
XLA Modules:
  0.0 126.7 jit_solution(1383738828088266944)
XLA Ops:
  0.6 1.2 convert_bitcast_fusion.off_ref
  1.8 1.4 %copy.7.ocol_ref = s32[64,1]{1,0:T(8,128)} copy(s32[64,1]{0,1:T(1,128)} %param.6) | data formatting | bytes 512 | tf_op args[2]
  3.2 107.5 %assemble_and_reduce.1 = (f32[384,4096]{1,0:T(8,128)}, f32[512,4096]{1,0:T(8,128)}, f32[384,512]{1,0:T(8,128)}, f32[512,512]{1,0:T(8,128)}) custom-call(f32[64,4096]{1,0:T(8,128)} %child_ref.1, s32[64,1]{1,0:T(8,128)} %copy.7.ocol_ref, s32[1,64]{1,0:T(1,128)} %bitcast.3, f32[1,64]{1,0:T(1,128)} %convert_bitcast_fusion.off_ref, f32[384,4096]{1,0:T(8,128)} %front_ref.1), custom_call_target="tpu_custom_call" | custom-call | tf_op jit(solution)/shard_map/assemble_and_reduce/pallas_call | solution.py:595
  110.7 16.0 %project_out.1 = (f32[512,4096]{1,0:T(8,128)}, f32[384,4096]{1,0:T(8,128)}, f32[384,512]{1,0:T(8,128)}) custom-call(f32[384,512]{1,0:T(8,128)} %get-tuple-element.7.basis_ref, f32[512,512]{1,0:T(8,128)} %get-tuple-element.8.linv_ref, f32[512,4096]{1,0:T(8,128)} %get-tuple-element.9.s_ref, f32[384,4096]{1,0:T(8,128)} %get-tuple-element.10.w_ref), custom_call_target="tpu_custom_call" | custom-call | tf_op jit(solution)/shard_map/project_out/pallas_call | solution.py:665

commit v6 on v5

--- a/solution.py
+++ b/solution.py
@@ -118,7 +118,7 @@
 
 
 def main_kernel(
-    child_ref, ocol_ref, orow_ref, off_ref, front_ref,
+    child_ref, orow_ref, off_ref, front_ref,
     w_out, f_out, q_ref, linv_ref,
     w_ref, f_ref, p_ref, a1_ref, a1_full, ah, al, r0, r1, r2, g_ref, dblk, xblk,
     outbox, inbox, zbox, onehot,
@@ -168,10 +168,11 @@
         pl.semaphore_signal(barrier, inc=1, device_id={"col": peer}, device_id_type=MESH)
 
     orow = orow_ref[...]
-    earlier = lax.broadcasted_iota(jnp.int32, (kids, kids), 0) < lax.broadcasted_iota(
-        jnp.int32, (kids, kids), 1
-    )
-    same = jnp.logical_and(ocol_ref[...] == orow, earlier)
+    owner = orow.astype(F32)
+    kid_down = lax.broadcasted_iota(jnp.int32, (kids, kids), 0)
+    kid_over = lax.broadcasted_iota(jnp.int32, (kids, kids), 1)
+    owner_down = jnp.sum(jnp.where(kid_down == kid_over, owner, 0.0), axis=1, keepdims=True)
+    same = jnp.logical_and(owner_down == owner, kid_down < kid_over)
     rank = jnp.sum(jnp.where(same, 1.0, 0.0), axis=0, keepdims=True).astype(jnp.int32)
     slot = orow * 8 + rank * 2
     boxes = 8 * count
@@ -179,7 +180,7 @@
     even = jnp.where(box_id == slot, 1.0, 0.0)
     odd = jnp.where(box_id == slot + 1, 1.0, 0.0)
     filled = even + odd
-    offset = jnp.sum(filled * off_ref[...], axis=1, keepdims=True)
+    offset = jnp.sum(filled * off_ref[...].astype(F32), axis=1, keepdims=True)
     offset = offset + jnp.sum(filled, axis=1, keepdims=True) - 1.0
     outbox[:, pl.ds(0, TAG)] = jnp.broadcast_to(offset, (boxes, TAG))
     choose = jnp.concatenate([even, odd], axis=1).astype(BF16)
@@ -546,7 +547,7 @@
         q_ref[...] = tdot(a1_full[...], linv_ref[...])
 
     steps = [(GRAM_TAU[p], 0, p) for p in range(7)]
-    steps += [(2 * p + c - 1, c, p) for c in range(1, n) for p in (0, 1, 2, 3, 5, 7, 8, 9, 10)]
+    steps += [(1.5 * p + 0.75 * c - 1, c, p) for c in range(1, n) for p in (0, 1, 2, 3, 5, 7, 8, 9, 10)]
     before = None
     ready = False
     for tau, c, p in sorted(steps):
@@ -600,7 +601,7 @@
             jax.ShapeDtypeStruct((rows, WIDE), F32),
             jax.ShapeDtypeStruct((WIDE, WIDE), F32),
         ),
-        in_specs=[vm, vm, vm, vm, hbm],
+        in_specs=[vm, vm, vm, hbm],
         out_specs=(hbm, hbm, vm, vm),
         scratch_shapes=[
             pltpu.VMEM((rows, cols), F32),
@@ -634,9 +635,8 @@
         name="assemble_and_reduce",
     )(
         child,
-        owner,
         owner.reshape(1, kids),
-        offset.reshape(1, kids).astype(F32),
+        offset.reshape(1, kids),
         front,
     )
 
@@ -659,7 +659,7 @@
 
 def tail(basis, linv, sums, w, scale):
     rows, cols = w.shape
-    tc = 512
+    tc = 1024
     whole = lambda size: pl.BlockSpec((size, WIDE), lambda i: (0, 0))
     tile = lambda size: pl.BlockSpec((size, tc), lambda i: (0, i))
     return pl.pallas_call(

time: 127 us -> 123 us (0.969)
  local copies, waits for them, and re-layouts: 1.36 us -> 0 us
    unnamed x1 -> x0, local copies, waits for them, and re-layouts: 1.36 us -> none
where the time goes in v6:
time: 123 us; the launch traced here: 122 us
  Pallas kernels  122 us (99%)
    pallas_call x1, Pallas kernels, all_reduced(): pl.pallas_call(main_kernel, out_shape=(jax.ShapeDtypeStruct((rows, cols),...  106 us
    pallas_call x1, Pallas kernels, tail(): pl.pallas_call(functools.partial(tail_kernel, scale), grid=(cols // tc,),...  15.4 us

profile of v6, /device:TPU:1, one launch (start us, length us, event | category | flops | bytes accessed | tf_op | source)
XLA Modules:
  0.0 122.3 jit_solution(15572810344980700192)
XLA Ops:
  0.6 106.3 %assemble_and_reduce.1 = (f32[384,4096]{1,0:T(8,128)}, f32[512,4096]{1,0:T(8,128)}, f32[384,512]{1,0:T(8,128)}, f32[512,512]{1,0:T(8,128)}) custom-call(f32[64,4096]{1,0:T(8,128)} %child_ref.1, s32[1,64]{1,0:T(1,128)} %bitcast.2, s32[1,64]{1,0:T(1,128)} %bitcast.3, f32[384,4096]{1,0:T(8,128)} %front_ref.1), custom_call_target="tpu_custom_call" | custom-call | tf_op jit(solution)/shard_map/assemble_and_reduce/pallas_call | solution.py:596
  106.9 15.4 %project_out.1 = (f32[512,4096]{1,0:T(8,128)}, f32[384,4096]{1,0:T(8,128)}, f32[384,512]{1,0:T(8,128)}) custom-call(f32[384,512]{1,0:T(8,128)} %get-tuple-element.7.basis_ref, f32[512,512]{1,0:T(8,128)} %get-tuple-element.8.linv_ref, f32[512,4096]{1,0:T(8,128)} %get-tuple-element.9.s_ref, f32[384,4096]{1,0:T(8,128)} %get-tuple-element.10.w_ref), custom_call_target="tpu_custom_call" | custom-call | tf_op jit(solution)/shard_map/project_out/pallas_call | solution.py:665
